TPU v7x, 32 devices: a whole 2x2x4 slice. The times are simulated.
32 devices in a mesh: dp: 4 (over y, x), wide: 8 (over z, core).
Axes of the slice: x: 2, y: 2, z: 4, core: 2. Of those that a mesh axis runs over, the one named last changes fastest.
Arguments:
- tokens: bfloat16 [36864, 768], P(('dp', 'wide')), may hold values from -6 to 6
- pos_index: int32 [36864, 2], P(('dp', 'wide')), may hold values from 0 to 196
- size_group: int32 [224], P(('dp', 'wide')), may hold values from 0 to 3, as said below
- pos_table: bfloat16 [197, 768], replicated, may hold values from -3 to 3
- prompts: float32 [50, 768], replicated, may hold values from -6 to 6
- norm_gains: float32 [2, 768], replicated, may hold values from 0.5 to 1.5
- w_qkv: bfloat16 [768, 2304], P('wide'), may hold values from -0.21875 to 0.21875
- w_out: bfloat16 [768, 768], P('wide'), may hold values from -1.75 to 1.75
- w_up: bfloat16 [768, 3072], P('wide'), may hold values from -0.21875 to 0.21875
- w_down: bfloat16 [3072, 768], P('wide'), may hold values from -0.109375 to 0.109375
- cotangent: bfloat16 [36864, 768], P(('dp', 'wide')), may hold values from -6 to 6
Outputs:
- outputs: bfloat16 [36864, 768], P(('dp', 'wide'))
- input_grad: bfloat16 [36864, 768], P(('dp', 'wide'))
- prompt_grad: float32 [50, 768], replicated
- penalty: float32 [], replicated
Inputs may be any that keep to these rules, and one draw needn't show every extreme that they name: `size_group`: 0, 1, 2 name images of 100, 196, 576 patches, 3 an empty slot; the images of one device's 7 slots take at most 1139 of its 1152 rows, and the last device's take exactly that.
All inputs are finite; a program needn't handle non-finite values.
Results may differ from a plain program's by a relative error of at most 0.013.
Values may be sent and summed in bfloat16 or wider, within the bound.
A program may use at most 192 MiB of HBM per device.

v0:
```python
import jax
import jax.numpy as jnp
from jax import lax
from jax.sharding import PartitionSpec as P

HEADS = 12
HEAD_DIM = 64
PROMPTS = 50
PATCH_S = 100
PATCH_M = 196
PATCH_L = 576
TOK_DEV = 1152


EPSILON = 1e-06
PENALTY_RATE = 3e-05


def layout(groups):
    patches = jnp.where(groups == 0, PATCH_S, jnp.where(groups == 1, PATCH_M, PATCH_L))
    lengths = jnp.where(groups == 3, 0, 1 + PROMPTS + patches).astype(jnp.int32)
    starts = jnp.cumsum(lengths) - lengths
    row_ids = jnp.arange(TOK_DEV, dtype=jnp.int32)
    inside = (row_ids[None, :] >= starts[:, None]) & (
        row_ids[None, :] < (starts + lengths)[:, None]
    )
    slot_number = jnp.arange(groups.shape[0], dtype=jnp.int32)
    segment = jnp.sum(jnp.where(inside, slot_number[:, None] + 1, 0), axis=0) - 1
    position = row_ids - jnp.sum(jnp.where(inside, starts[:, None], 0), axis=0)
    live_rows = segment >= 0
    prompt_slot = jnp.where(live_rows & (position >= 1) & (position <= PROMPTS), position - 1, -1)
    return (segment, prompt_slot, live_rows, lengths)


def layer_norm(values, gain):
    centered = values - jnp.mean(values, axis=-1, keepdims=True)
    return (
        centered * lax.rsqrt(jnp.mean(centered * centered, axis=-1, keepdims=True) + EPSILON) * gain
    )


def shards(
    tokens,
    pos_index,
    size_group,
    pos_table,
    prompts,
    norm_gains,
    w_qkv,
    w_out,
    w_up,
    w_down,
    cotangent,
):
    row_count = tokens.shape[0]
    model_width = tokens.shape[1]
    head_count = HEADS
    head_dim = HEAD_DIM
    block_heads = 4
    block_count = head_count // block_heads
    score_scale = head_dim ** (-0.5)
    prompt_count = prompts.shape[0]
    segment, prompt_slot, live_rows, lengths = layout(size_group)
    image_starts = jnp.cumsum(lengths) - lengths
    positions = jnp.arange(pos_table.shape[0], dtype=jnp.int32)
    twohot = (
        0.5 * (pos_index[:, 0:1] == positions[None, :]).astype(jnp.float32)
        + 0.5 * (pos_index[:, 1:2] == positions[None, :]).astype(jnp.float32)
    ).astype(jnp.bfloat16)
    pos_shift = jnp.dot(twohot, pos_table, preferred_element_type=jnp.float32)
    chosen = jnp.take(prompts, jnp.maximum(prompt_slot, 0), axis=0)
    is_prompt = (prompt_slot >= 0)[:, None]
    hidden_in = jnp.where(is_prompt, chosen, tokens.astype(jnp.float32) + pos_shift)
    full_qkv, full_out, full_up, full_down = (
        lax.all_gather(w_qkv, "wide", axis=0, tiled=True),
        lax.all_gather(w_out, "wide", axis=0, tiled=True),
        lax.all_gather(w_up, "wide", axis=0, tiled=True),
        lax.all_gather(w_down, "wide", axis=0, tiled=True),
    )
    normed, first_pull = jax.vjp(lambda t: layer_norm(t, norm_gains[0]), hidden_in)
    joint_qkv = jnp.dot(
        normed.astype(jnp.bfloat16), full_qkv, preferred_element_type=jnp.float32
    ).astype(jnp.bfloat16)
    head_split = joint_qkv.reshape(row_count, 3, head_count, head_dim).transpose(1, 2, 0, 3)
    head_blocks = head_split.reshape(3, block_count, block_heads, row_count, head_dim)
    same_image = (segment[:, None] == segment[None, :])[None]

    def attend(pieces):
        queries, key_rows, value_rows = pieces
        scores = (
            jnp.einsum("hqd,hkd->hqk", queries, key_rows, preferred_element_type=jnp.float32)
            * score_scale
        )
        scores = jnp.where(same_image, scores, -1e30)
        peak_score = jnp.max(scores, axis=-1, keepdims=True)
        exponent = jnp.exp(scores - peak_score)
        totals = jnp.sum(exponent, axis=-1, keepdims=True)
        attn_weights = (exponent / totals).astype(jnp.bfloat16)
        result = jnp.einsum(
            "hqk,hkd->hqd", attn_weights, value_rows, preferred_element_type=jnp.float32
        )
        return (result, (peak_score + jnp.log(totals))[:, :, 0])

    mixed_heads, log_total = lax.map(attend, (head_blocks[0], head_blocks[1], head_blocks[2]))
    mixed_heads = (
        mixed_heads.reshape(head_count, row_count, head_dim)
        .transpose(1, 0, 2)
        .reshape(row_count, model_width)
        .astype(jnp.bfloat16)
    )
    middle = hidden_in + jnp.dot(mixed_heads, full_out, preferred_element_type=jnp.float32)
    second, second_pull = jax.vjp(lambda t: layer_norm(t, norm_gains[1]), middle)
    inner_act = jnp.dot(second.astype(jnp.bfloat16), full_up, preferred_element_type=jnp.float32)
    activated, gelu_pull = jax.vjp(lambda t: jax.nn.gelu(t, approximate=False), inner_act)
    live_float = live_rows[:, None].astype(jnp.float32)
    outputs = (
        (
            middle
            + jnp.dot(activated.astype(jnp.bfloat16), full_down, preferred_element_type=jnp.float32)
        )
        * live_float
    ).astype(jnp.bfloat16)
    full_qkv, full_out, full_up, full_down = (
        lax.all_gather(w_qkv, "wide", axis=0, tiled=True),
        lax.all_gather(w_out, "wide", axis=0, tiled=True),
        lax.all_gather(w_up, "wide", axis=0, tiled=True),
        lax.all_gather(w_down, "wide", axis=0, tiled=True),
    )
    masked_cot = cotangent * live_rows[:, None].astype(jnp.bfloat16)
    out_grad = masked_cot.astype(jnp.float32)
    act_grad = jnp.einsum("td,fd->tf", masked_cot, full_down, preferred_element_type=jnp.float32)
    inner_grad = gelu_pull(act_grad)[0].astype(jnp.bfloat16)
    second_grad = jnp.einsum("tf,df->td", inner_grad, full_up, preferred_element_type=jnp.float32)
    middle_grad = out_grad + second_pull(second_grad)[0]
    mixed_grad = jnp.einsum(
        "te,de->td", middle_grad.astype(jnp.bfloat16), full_out, preferred_element_type=jnp.float32
    ).astype(jnp.bfloat16)
    mixed_split = (
        mixed_grad.reshape(row_count, head_count, head_dim)
        .transpose(1, 0, 2)
        .reshape(block_count, block_heads, row_count, head_dim)
    )

    def attend_back(pieces):
        queries, key_rows, value_rows, head_grad, head_total = pieces
        scores = (
            jnp.einsum("hqd,hkd->hqk", queries, key_rows, preferred_element_type=jnp.float32)
            * score_scale
        )
        scores = jnp.where(same_image, scores, -1e30)
        attn_probs = jnp.exp(scores - head_total[:, :, None])
        value_grad = jnp.einsum(
            "hqk,hqd->hkd",
            attn_probs.astype(jnp.bfloat16),
            head_grad,
            preferred_element_type=jnp.float32,
        )
        prob_grad = jnp.einsum(
            "hqd,hkd->hqk", head_grad, value_rows, preferred_element_type=jnp.float32
        )
        score_grad = (
            attn_probs * (prob_grad - jnp.sum(prob_grad * attn_probs, axis=-1, keepdims=True))
        ).astype(jnp.bfloat16)
        query_grad = (
            jnp.einsum("hqk,hkd->hqd", score_grad, key_rows, preferred_element_type=jnp.float32)
            * score_scale
        )
        key_grad = (
            jnp.einsum("hqk,hqd->hkd", score_grad, queries, preferred_element_type=jnp.float32)
            * score_scale
        )
        return jnp.stack((query_grad, key_grad, value_grad))

    joint_grad = lax.map(
        attend_back, (head_blocks[0], head_blocks[1], head_blocks[2], mixed_split, log_total)
    )
    joint_grad = joint_grad.transpose(1, 0, 2, 3, 4).reshape(3, head_count, row_count, head_dim)
    joint_flat = (
        joint_grad.transpose(2, 0, 1, 3).reshape(row_count, 3 * model_width).astype(jnp.bfloat16)
    )
    normed_grad = jnp.einsum("tc,dc->td", joint_flat, full_qkv, preferred_element_type=jnp.float32)
    hidden_grad = middle_grad + first_pull(normed_grad)[0]
    input_grad = jnp.where(is_prompt, 0.0, hidden_grad).astype(jnp.bfloat16)

    def add_image(total, image_number):
        begin = image_starts[image_number] + 1
        taken = lax.dynamic_slice_in_dim(hidden_grad, begin, prompt_count, 0)
        weight = (lengths[image_number] > 0).astype(jnp.float32)
        return (total + weight * taken, None)

    prompt_local, _ = lax.scan(
        add_image,
        jnp.zeros((prompt_count, model_width), jnp.float32),
        jnp.arange(lengths.shape[0], dtype=jnp.int32),
    )
    count_local = jnp.sum(lengths).astype(jnp.float32)
    token_total = lax.psum(count_local, ("dp", "wide"))
    share = lax.psum_scatter(prompt_local, ("dp", "wide"), scatter_dimension=1, tiled=True)
    share_width = share.shape[1]
    own_prompts = lax.dynamic_slice_in_dim(
        prompts, lax.axis_index(("dp", "wide")) * share_width, share_width, 1
    )
    pen_rate = 2.0 * PENALTY_RATE * token_total / (prompt_count * model_width)
    prompt_grad = lax.all_gather(share + pen_rate * own_prompts, ("dp", "wide"), axis=1, tiled=True)
    penalty = PENALTY_RATE * token_total * jnp.mean(prompts * prompts)
    return (outputs, input_grad, prompt_grad, penalty)


def solution(mesh):
    return jax.shard_map(
        shards,
        mesh=mesh,
        in_specs=(
            P(("dp", "wide"), None),
            P(("dp", "wide"), None),
            P(("dp", "wide")),
            P(),
            P(),
            P(),
            P("wide", None),
            P("wide", None),
            P("wide", None),
            P("wide", None),
            P(("dp", "wide"), None),
        ),
        out_specs=(P(("dp", "wide"), None), P(("dp", "wide"), None), P(), P()),
        check_vma=False,
    )
```

profile of v0, /device:TPU:0, one launch (start us, length us, event | category | flops | bytes accessed | tf_op | source)
XLA Modules:
  0.0 702.0 jit_solution(15730844023392227863)
XLA Ops:
  37.4 42.2 %psum.7 = f32[]{:T(128)} all-reduce(f32[]{:T(128)S(6)} %convert_element_type.125), channel_id=1, replica_groups=mesh['dp'=4,'wide'=8] {'dp','wide'}, use_global_device_ids=true, to_apply=%region_22.23 | all-reduce | flops 1 | bytes 8 | tf_op jit(solution)/shard_map/psum | solution.py:197
  81.6 9.9 %convolution_convert_fusion = bf16[1152,2304]{1,0:T(8,128)(2,1)} fusion(bf16[768,2304]{1,0:T(8,128)(2,1)} %all-gather.5.cloned.1.call-done, f32[1152,768]{0,1:T(8,128)} %copy-done.6, f32[768]{0:T(1024)S(1)} %get-tuple-element.265, f32[1152]{0:T(1024)S(1)} %fusion.80, f32[1152]{0:T(1024)S(1)} %broadcast_multiply_fusion.1), kind=kOutput, calls=%fused_computation.76 | convolution fusion | flops 4083056640 | bytes 12398592 | tf_op jit(solution)/shard_map/dot_general | solution.py:81
  105.2 78.5 %while.37 = (s32[]{:T(128)}, bf16[3,4,1152,64]{2,3,1,0:T(8,128)(2,1)}, f32[3,4,1152]{2,1,0:T(4,128)S(1)}, bf16[3,4,1152,64]{2,3,1,0:T(8,128)(2,1)}, bf16[3,4,115...) while((s32[]{:T(128)}, ...), condition=%wide.region_8.9_spmd.clone, body=%wide.region_5.8_spmd.clone.sunk | while | flops 1402744320 | bytes 168549040 | solution.py:104
  119.1 11.1 %fusion.135 = bf16[3,4,1152,64]{2,3,1,0:T(8,128)(2,1)S(1)} fusion(bf16[3,4,1152,64]{2,3,1,0:T(8,128)(2,1)S(1)} %copy-done.39, s32[]{:T(128)S(6)} %copy.96, f32[4,1152,1152]{1,2,0:T(8,128)} %copy-done.3, f32[4,1152]{1,0:T(4,128)S(1)} %fusion.134, f32[4,1152]{1,0:T(4,128)S(1)} %get-tuple-element.458, bf16[3,4,1152,64]{2,3,1,0:T(8,128)(2,1)} %get-tuple-element.496), kind=kOutput, calls=%fused_computation.11.clone.1 | convolution fusion | flops 695402496 | bytes 23041024 | tf_op jit(solution)/shard_map/while/body/eval_jaxpr/hqk,hkd->hqd/dot_general | solution.py:99
  145.2 11.2 %fusion.135 = bf16[3,4,1152,64]{2,3,1,0:T(8,128)(2,1)S(1)} fusion(bf16[3,4,1152,64]{2,3,1,0:T(8,128)(2,1)S(1)} %copy-done.39, s32[]{:T(128)S(6)} %copy.96, f32[4,1152,1152]{1,2,0:T(8,128)} %copy-done.3, f32[4,1152]{1,0:T(4,128)S(1)} %fusion.134, f32[4,1152]{1,0:T(4,128)S(1)} %get-tuple-element.458, bf16[3,4,1152,64]{2,3,1,0:T(8,128)(2,1)} %get-tuple-element.496), kind=kOutput, calls=%fused_computation.11.clone.1 | convolution fusion | flops 695402496 | bytes 23041024 | tf_op jit(solution)/shard_map/while/body/eval_jaxpr/hqk,hkd->hqd/dot_general | solution.py:99
  171.3 11.1 %fusion.135 = bf16[3,4,1152,64]{2,3,1,0:T(8,128)(2,1)S(1)} fusion(bf16[3,4,1152,64]{2,3,1,0:T(8,128)(2,1)S(1)} %copy-done.39, s32[]{:T(128)S(6)} %copy.96, f32[4,1152,1152]{1,2,0:T(8,128)} %copy-done.3, f32[4,1152]{1,0:T(4,128)S(1)} %fusion.134, f32[4,1152]{1,0:T(4,128)S(1)} %get-tuple-element.458, bf16[3,4,1152,64]{2,3,1,0:T(8,128)(2,1)} %get-tuple-element.496), kind=kOutput, calls=%fused_computation.11.clone.1 | convolution fusion | flops 695402496 | bytes 23041024 | tf_op jit(solution)/shard_map/while/body/eval_jaxpr/hqk,hkd->hqd/dot_general | solution.py:99
  190.6 39.3 %fusion.48 = (f32[1152,3072]{1,0:T(8,128)}, f32[1152,3072]{1,0:T(8,128)}) fusion(bf16[768,3072]{1,0:T(8,128)(2,1)} %all-gather.9.cloned.1.call-done, f32[1152,768]{0,1:T(8,128)} %copy-done.10, f32[768]{0:T(1024)S(1)} %copy-done.35, f32[1152]{0:T(1024)S(1)} %fusion.81, f32[1152]{0:T(1024)S(1)} %broadcast_multiply_fusion), kind=kOutput, calls=%fused_computation.60 | convolution fusion | flops 5658771456 | bytes 36581376 | tf_op jit(solution)/shard_map/dot_general | solution.py:113
  229.9 23.7 %multiply_reduce_fusion.2 = (f32[1152]{0:T(1024)S(1)}, f32[1152,768]{0,1:T(8,128)}) fusion(f32[1152,768]{0,1:T(8,128)} %copy-done.10, f32[1152]{0:T(1024)S(1)} %broadcast_multiply_fusion, f32[768]{0:T(1024)S(1)} %copy-done.35, bf16[768,3072]{1,0:T(8,128)(2,1)} %all-gather.9.cloned.1.call-done, f32[1152,3072]{1,0:T(8,128)} %get-tuple-element.332, ...), kind=kOutput, calls=%fused_computation.92 | convolution fusion | flops 10925603840 | bytes 46610688 | tf_op jit(solution)/shard_map/tf,df->td/dot_general | solution.py:133
  259.5 198.0 %while.38 = (s32[]{:T(128)}, bf16[3,3,4,1152,64]{3,4,2,0,1:T(8,128)(2,1)}, bf16[3,4,1152,64]{2,3,1,0:T(8,128)(2,1)}, bf16[3,4,1152,64]{2,3,1,0:T(8,128)(2,1)}, f...) while((s32[]{:T(128)}, ...), condition=%wide.region_15.16_spmd.clone, body=%wide.region_13.15_spmd.clone.sunk | while | flops 3452972544 | bytes 190317296 | solution.py:174
  260.5 13.6 %fusion.144 = f32[4,1152,1152]{1,2,0:T(8,128)} fusion(f32[4,1152]{1,0:T(4,128)S(1)} %dynamic-slice_bitcast_fusion.2, pred[1152,1152]{0,1:T(8,128)(4,1)S(1)} %compare_bitcast_fusion.5, bf16[3,4,1152,64]{2,3,1,0:T(8,128)(2,1)} %get-tuple-element.520, s32[]{:T(128)S(6)} %copy.104, bf16[3,4,1152,64]{2,3,1,0:T(8,128)(2,1)} %get-tuple-element.519), kind=kOutput, calls=%fused_computation.24.clone.1 | convolution fusion | flops 695402496 | bytes 23759872 | tf_op jit(solution)/shard_map/while/body/eval_jaxpr/hqd,hkd->hqk/dot_general | solution.py:147
  274.1 9.9 %fusion.145 = bf16[1,4,1152,64]{2,3,1,0:T(8,128)(2,1)} fusion(f32[4,1152,1152]{1,2,0:T(8,128)} %fusion.144, bf16[3,4,1152,64]{2,3,1,0:T(8,128)(2,1)S(1)} %get-tuple-element.522, s32[]{:T(128)S(6)} %copy.104), kind=kOutput, calls=%fused_computation.35.clone.1 | convolution fusion | flops 684785664 | bytes 22413316 | tf_op jit(solution)/shard_map/while/body/eval_jaxpr/hqk,hqd->hkd/dot_general | solution.py:152
  284.0 17.3 %multiply_reduce_fusion.7 = (f32[4,1152]{1,0:T(4,128)S(1)}, f32[4,1152,1152]{1,2,0:T(8,128)}) fusion(f32[4,1152,1152]{1,2,0:T(8,128)} %fusion.144, bf16[3,4,1152,64]{2,3,1,0:T(8,128)(2,1)} %get-tuple-element.523, s32[]{:T(128)S(6)} %copy.104, bf16[3,4,1152,64]{2,3,1,0:T(8,128)(2,1)S(1)} %get-tuple-element.522), kind=kOutput, calls=%fused_computation.26.clone.1 | convolution fusion | flops 690089472 | bytes 43666432 | tf_op jit(solution)/shard_map/while/body/eval_jaxpr/hqd,hkd->hqk/dot_general | solution.py:158
  301.3 13.9 %multiply_convert_fusion.14 = bf16[4,1152,1152]{1,2,0:T(8,128)(2,1)S(1)} fusion(f32[4,1152,1152]{1,2,0:T(8,128)} %fusion.144, f32[4,1152,1152]{1,2,0:T(8,128)} %get-tuple-element.467, f32[4,1152]{1,0:T(4,128)S(1)} %get-tuple-element.468), kind=kLoop, calls=%fused_computation.25.clone.1 | loop fusion | flops 15925248 | bytes 53102592 | tf_op jit(solution)/shard_map/while/body/eval_jaxpr/convert_element_type | solution.py:163
  326.4 13.6 %fusion.144 = f32[4,1152,1152]{1,2,0:T(8,128)} fusion(f32[4,1152]{1,0:T(4,128)S(1)} %dynamic-slice_bitcast_fusion.2, pred[1152,1152]{0,1:T(8,128)(4,1)S(1)} %compare_bitcast_fusion.5, bf16[3,4,1152,64]{2,3,1,0:T(8,128)(2,1)} %get-tuple-element.520, s32[]{:T(128)S(6)} %copy.104, bf16[3,4,1152,64]{2,3,1,0:T(8,128)(2,1)} %get-tuple-element.519), kind=kOutput, calls=%fused_computation.24.clone.1 | convolution fusion | flops 695402496 | bytes 23759872 | tf_op jit(solution)/shard_map/while/body/eval_jaxpr/hqd,hkd->hqk/dot_general | solution.py:147
  339.9 9.9 %fusion.145 = bf16[1,4,1152,64]{2,3,1,0:T(8,128)(2,1)} fusion(f32[4,1152,1152]{1,2,0:T(8,128)} %fusion.144, bf16[3,4,1152,64]{2,3,1,0:T(8,128)(2,1)S(1)} %get-tuple-element.522, s32[]{:T(128)S(6)} %copy.104), kind=kOutput, calls=%fused_computation.35.clone.1 | convolution fusion | flops 684785664 | bytes 22413316 | tf_op jit(solution)/shard_map/while/body/eval_jaxpr/hqk,hqd->hkd/dot_general | solution.py:152
  349.9 17.3 %multiply_reduce_fusion.7 = (f32[4,1152]{1,0:T(4,128)S(1)}, f32[4,1152,1152]{1,2,0:T(8,128)}) fusion(f32[4,1152,1152]{1,2,0:T(8,128)} %fusion.144, bf16[3,4,1152,64]{2,3,1,0:T(8,128)(2,1)} %get-tuple-element.523, s32[]{:T(128)S(6)} %copy.104, bf16[3,4,1152,64]{2,3,1,0:T(8,128)(2,1)S(1)} %get-tuple-element.522), kind=kOutput, calls=%fused_computation.26.clone.1 | convolution fusion | flops 690089472 | bytes 43666432 | tf_op jit(solution)/shard_map/while/body/eval_jaxpr/hqd,hkd->hqk/dot_general | solution.py:158
  367.2 13.9 %multiply_convert_fusion.14 = bf16[4,1152,1152]{1,2,0:T(8,128)(2,1)S(1)} fusion(f32[4,1152,1152]{1,2,0:T(8,128)} %fusion.144, f32[4,1152,1152]{1,2,0:T(8,128)} %get-tuple-element.467, f32[4,1152]{1,0:T(4,128)S(1)} %get-tuple-element.468), kind=kLoop, calls=%fused_computation.25.clone.1 | loop fusion | flops 15925248 | bytes 53102592 | tf_op jit(solution)/shard_map/while/body/eval_jaxpr/convert_element_type | solution.py:163
  392.3 13.6 %fusion.144 = f32[4,1152,1152]{1,2,0:T(8,128)} fusion(f32[4,1152]{1,0:T(4,128)S(1)} %dynamic-slice_bitcast_fusion.2, pred[1152,1152]{0,1:T(8,128)(4,1)S(1)} %compare_bitcast_fusion.5, bf16[3,4,1152,64]{2,3,1,0:T(8,128)(2,1)} %get-tuple-element.520, s32[]{:T(128)S(6)} %copy.104, bf16[3,4,1152,64]{2,3,1,0:T(8,128)(2,1)} %get-tuple-element.519), kind=kOutput, calls=%fused_computation.24.clone.1 | convolution fusion | flops 695402496 | bytes 23759872 | tf_op jit(solution)/shard_map/while/body/eval_jaxpr/hqd,hkd->hqk/dot_general | solution.py:147
  415.7 17.3 %multiply_reduce_fusion.7 = (f32[4,1152]{1,0:T(4,128)S(1)}, f32[4,1152,1152]{1,2,0:T(8,128)}) fusion(f32[4,1152,1152]{1,2,0:T(8,128)} %fusion.144, bf16[3,4,1152,64]{2,3,1,0:T(8,128)(2,1)} %get-tuple-element.523, s32[]{:T(128)S(6)} %copy.104, bf16[3,4,1152,64]{2,3,1,0:T(8,128)(2,1)S(1)} %get-tuple-element.522), kind=kOutput, calls=%fused_computation.26.clone.1 | convolution fusion | flops 690089472 | bytes 43666432 | tf_op jit(solution)/shard_map/while/body/eval_jaxpr/hqd,hkd->hqk/dot_general | solution.py:158
  433.0 13.9 %multiply_convert_fusion.14 = bf16[4,1152,1152]{1,2,0:T(8,128)(2,1)S(1)} fusion(f32[4,1152,1152]{1,2,0:T(8,128)} %fusion.144, f32[4,1152,1152]{1,2,0:T(8,128)} %get-tuple-element.467, f32[4,1152]{1,0:T(4,128)S(1)} %get-tuple-element.468), kind=kLoop, calls=%fused_computation.25.clone.1 | loop fusion | flops 15925248 | bytes 53102592 | tf_op jit(solution)/shard_map/while/body/eval_jaxpr/convert_element_type | solution.py:163
  478.2 46.8 %while.39 = (s32[]{:T(128)}, f32[50,768]{1,0:T(8,128)S(1)}, s32[7]{0:T(128)S(1)}, s32[7]{0:T(128)S(1)}, s32[7]{0:T(128)S(1)}, /*index=5*/f32[1152,768]{1,0:T(8,1...) while((s32[]{:T(128)}, f32[50,768]{1,0:T(8,128)S(1)}, ...), condition=%wide.region_19.20_spmd.clone, body=%wide.region_18.19_spmd.clone.sunk | while | flops 115212 | bytes 461073 | solution.py:191
  525.7 18.1 %fusion.59 = bf16[1152,768]{0,1:T(8,128)(2,1)} fusion(f32[1152,768]{0,1:T(8,128)} %copy-done.10, bf16[3072,768]{1,0:T(8,128)(2,1)} %all-gather.11.cloned.1.call-done, f32[1152,3072]{1,0:T(8,128)} %get-tuple-element.332, f32[1152,3072]{1,0:T(8,128)} %get-tuple-element.333, f32[1152]{0:T(1024)S(1)} %copy-done.31), kind=kOutput, calls=%fused_computation.98 | convolution fusion | flops 5449089024 | bytes 38343168 | tf_op jit(solution)/shard_map/dot_general | solution.py:119
  549.9 98.4 %all-reduce.3.cloned.1.call-done = f32[50,768]{1,0:T(8,128)} async-done(((f32[50,768]{1,0:T(8,128)}), f32[50,768]{1,0:T(8,128)}) %all-reduce.3.cloned.1.call-update) | async-done | bytes 153616
  649.3 44.0 %all_gather.23 = f32[50,768]{0,1:T(8,128)S(1)} all-gather(f32[50,24]{0,1:T(8,128)S(1)} %copy.68), channel_id=1, replica_groups=mesh['dp'=4,'wide'=8] {'dp','wide'}, dimensions={1}, use_global_device_ids=true | all-gather | bytes 158400 | tf_op jit(solution)/shard_map/all_gather | solution.py:204
  (231 shorter events, 192.3 us)
Async XLA Ops:
  7.2 21.0 %copy-start = (bf16[197,768]{1,0:T(8,128)(2,1)S(1)}, bf16[197,768]{1,0:T(8,128)(2,1)}, u32[]{:S(2)}) copy-start(bf16[197,768]{1,0:T(8,128)(2,1)} %param.20) | copy-start | bytes 907780
  7.2 9.7 %copy-start.2 = (f32[50,768]{1,0:T(8,128)S(1)}, f32[50,768]{1,0:T(8,128)}, u32[]{:S(2)}) copy-start(f32[50,768]{1,0:T(8,128)} %param.21) | copy-start | bytes 460804
  7.2 74.3 %all-gather.5.cloned.1.call-start = ((), (), s32[]{:S(2)}) async-start(), calls=%async_computation | async-start | bytes 3981312 | tf_op jit(solution)/shard_map/all_gather | solution.py:75
  7.9 175.8 %all-gather.7.cloned.1.call-start = ((), (), s32[]{:S(2)}) async-start(), calls=%async_computation.1 | async-start | bytes 1327104 | tf_op jit(solution)/shard_map/all_gather | solution.py:76
  8.7 181.9 %all-gather.9.cloned.1.call-start = ((), (), s32[]{:S(2)}) async-start(), calls=%async_computation.2 | async-start | bytes 5308416 | tf_op jit(solution)/shard_map/all_gather | solution.py:77
  9.4 220.5 %all-gather.11.cloned.1.call-start = ((), (), s32[]{:S(2)}) async-start(), calls=%async_computation.3 | async-start | bytes 5308416 | tf_op jit(solution)/shard_map/all_gather | solution.py:78
  10.0 638.3 %all-reduce.3.cloned.1.call-start = ((), (), s32[]{:S(2)}) async-start(), calls=%async_computation.4 | async-start | bytes 344064
  13.2 14.9 %copy-start.27 = (pred[1152]{0:T(1024)(128)(4,1)}, pred[1152]{0:T(1024)(128)(4,1)S(1)}, u32[]{:S(2)}) copy-start(pred[1152]{0:T(1024)(128)(4,1)S(1)} %get-tuple-element.325) | copy-start | bytes 3460
  28.1 53.4 %copy-start.33 = (f32[768]{0:T(1024)}, f32[768]{0:T(1024)S(1)}, u32[]{:S(2)}) copy-start(f32[768]{0:T(1024)S(1)} %get-tuple-element.265) | copy-start | bytes 9220
  31.7 49.9 %copy-start.19 = (f32[1152]{0:T(1024)}, f32[1152]{0:T(1024)S(1)}, u32[]{:S(2)}) copy-start(f32[1152]{0:T(1024)S(1)} %broadcast_multiply_fusion.1) | copy-start | bytes 13828
  33.9 57.6 %copy-start.23 = (f32[1152]{0:T(1024)}, f32[1152]{0:T(1024)S(1)}, u32[]{:S(2)}) copy-start(f32[1152]{0:T(1024)S(1)} %multiply_reduce_fusion.4) | copy-start | bytes 13828
  34.4 57.1 %copy-start.21 = (f32[1152]{0:T(1024)}, f32[1152]{0:T(1024)S(1)}, u32[]{:S(2)}) copy-start(f32[1152]{0:T(1024)S(1)} %fusion.80) | copy-start | bytes 13828
  190.6 39.3 %copy-start.13 = (bf16[1152,768]{0,1:T(8,128)(2,1)S(1)}, bf16[1152,768]{0,1:T(8,128)(2,1)}, u32[]{:S(2)}) copy-start(bf16[1152,768]{0,1:T(8,128)(2,1)} %copy.65) | copy-start | bytes 5308420
  190.6 39.3 %copy-start.29 = (bf16[1152]{0:T(1024)(128)(2,1)S(1)}, bf16[1152]{0:T(1024)(128)(2,1)}, u32[]{:S(2)}) copy-start(bf16[1152]{0:T(1024)(128)(2,1)} %get-tuple-element.316) | copy-start | bytes 6916
  259.4 198.1 %copy-start.20 = (f32[1152]{0:T(1024)S(1)}, f32[1152]{0:T(1024)}, u32[]{:S(2)}) copy-start(f32[1152]{0:T(1024)} %copy-done.19) | copy-start | bytes 13828
  259.5 198.1 %copy-start.34 = (f32[768]{0:T(1024)S(1)}, f32[768]{0:T(1024)}, u32[]{:S(2)}) copy-start(f32[768]{0:T(1024)} %copy-done.33) | copy-start | bytes 9220
  259.6 24.3 %copy-start.8 = (bf16[3,4,1152,64]{2,3,1,0:T(8,128)(2,1)}, bf16[3,4,1152,64]{2,3,1,0:T(8,128)(2,1)S(1)}, u32[]{:S(2)}) copy-start(bf16[3,4,1152,64]{2,3,1,0:T(8,128)(2,1)S(1)} %get-tuple-element.522) | copy-start | bytes 5308420 | tf_op jit(solution)/shard_map/while
  325.6 24.3 %copy-start.8 = (bf16[3,4,1152,64]{2,3,1,0:T(8,128)(2,1)}, bf16[3,4,1152,64]{2,3,1,0:T(8,128)(2,1)S(1)}, u32[]{:S(2)}) copy-start(bf16[3,4,1152,64]{2,3,1,0:T(8,128)(2,1)S(1)} %get-tuple-element.522) | copy-start | bytes 5308420 | tf_op jit(solution)/shard_map/while
  391.4 24.3 %copy-start.8 = (bf16[3,4,1152,64]{2,3,1,0:T(8,128)(2,1)}, bf16[3,4,1152,64]{2,3,1,0:T(8,128)(2,1)S(1)}, u32[]{:S(2)}) copy-start(bf16[3,4,1152,64]{2,3,1,0:T(8,128)(2,1)S(1)} %get-tuple-element.522) | copy-start | bytes 5308420 | tf_op jit(solution)/shard_map/while
  457.5 9.6 %copy-start.24 = (f32[1152]{0:T(1024)S(1)}, f32[1152]{0:T(1024)}, u32[]{:S(2)}) copy-start(f32[1152]{0:T(1024)} %copy-done.23) | copy-start | bytes 13828
  457.5 9.6 %copy-start.7 = (f32[1152,768]{0,1:T(8,128)S(1)}, f32[1152,768]{0,1:T(8,128)}, u32[]{:S(2)}) copy-start(f32[1152,768]{0,1:T(8,128)} %copy-done.6) | copy-start | bytes 10616836
  457.6 9.6 %copy-start.22 = (f32[1152]{0:T(1024)S(1)}, f32[1152]{0:T(1024)}, u32[]{:S(2)}) copy-start(f32[1152]{0:T(1024)} %copy-done.21) | copy-start | bytes 13828
  473.0 52.8 %copy-start.31 = (f32[1152]{0:T(1024)S(1)}, f32[1152]{0:T(1024)}, u32[]{:S(2)}) copy-start(f32[1152]{0:T(1024)} %get-tuple-element.327) | copy-start | bytes 13828
  525.7 168.4 %copy-start.1 = (bf16[197,768]{1,0:T(8,128)(2,1)S(1)}, bf16[197,768]{1,0:T(8,128)(2,1)}, u32[]{:S(2)}) copy-start(bf16[197,768]{1,0:T(8,128)(2,1)} %param.20) | copy-start | bytes 907780
  (38 other events, 130.3 us)
Sparse Core Ops, SparseCore 0:
  9.7 44.2 all-gather.4
  55.6 21.7 all-gather.6
  79.0 51.4 all-gather.8
  132.0 50.5 all-gather.10
  525.8 122.3 all-reduce.2
where the time goes:
time: 711 us; the launch traced here: 702 us
  matrix products  306 us (43%)
  waiting for transfers between devices  101 us (14%)
  blocking collectives  86.2 us (12%)
  local copies, waits for them, and re-layouts  81.7 us (11%)
  other arithmetic  80.1 us (11%)
  loops' own time  28.3 us (4%)
  between operations  18.2 us (3%)
    unnamed x6, waiting for transfers between devices  101 us
    dot_general x3, matrix products, attend_back(): jnp.einsum('hqd,hkd->hqk', head_grad, value_rows, preferred_element_type=...  51.9 us
    all_gather x1, blocking collectives, shards(): lax.all_gather(share + pen_rate * own_prompts, ('dp', 'wide'), axis=1, ti...  44 us
    psum x1, blocking collectives, shards(): token_total = lax.psum(count_local, ('dp', 'wide'))  42.2 us
    convert_element_type x3, other arithmetic, attend_back(): score_grad = (attn_probs * (prob_grad - jnp.sum(prob_grad * attn_probs, a...  41.7 us
    dot_general x3, matrix products, attend_back(): jnp.einsum('hqd,hkd->hqk', queries, key_rows, preferred_element_type=jnp....  40.7 us
    dot_general x1, matrix products, shards(): jnp.dot(second.astype(jnp.bfloat16), full_up, preferred_element_type=jnp....  39.3 us
    dot_general x3, matrix products, attend(): jnp.einsum('hqk,hkd->hqd', attn_weights, value_rows, preferred_element_ty...  33.5 us
  transfers between devices with their start and end apart: 5, of which 1 were waited for; matrix products, arithmetic and copies ran while one was open for 25% of the time, Pallas kernels for 0%

commit v1 on v0

v1 whole, which is shorter than its diff:
```python
import functools

import jax
import jax.numpy as jnp
from jax import lax
from jax.experimental import pallas as pl
from jax.experimental.pallas import tpu as pltpu
from jax.sharding import PartitionSpec as P

HEADS = 12
HEAD_DIM = 64
PROMPTS = 50
PATCH_S = 100
PATCH_M = 196
PATCH_L = 576

EPSILON = 1e-06
PENALTY_RATE = 3e-05
SCALE = HEAD_DIM**-0.5
LOG2E = 1.4426950408889634
SCORE = SCALE * LOG2E

BF = jnp.bfloat16
F32 = jnp.float32
NN = (((1,), (0,)), ((), ()))
NT = (((1,), (1,)), ((), ()))
MESH = pl.DeviceIdType.MESH

LANES = 128
HEAD_COLS = 256
PAIRS = HEAD_COLS // LANES
GROUP_HEADS = HEAD_COLS // HEAD_DIM
SMALL = 256
LARGE = 640
CHUNKS = {SMAL: c for SMAL, c in ((SMALL, ((0, 256),)), (LARGE, ((0, 256), (256, 256), (512, 128))))}
POS_ROWS = 256
SLOT_ROWS = 64


def dot(a, b, dims=NN):
    return lax.dot_general(a, b, dims, preferred_element_type=F32)


def image_length(group):
    patches = jnp.where(group == 0, PATCH_S, jnp.where(group == 1, PATCH_M, PATCH_L))
    return jnp.where(group == 3, 0, 1 + PROMPTS + patches).astype(jnp.int32)


def total_length(groups, slots):
    total = jnp.int32(0)
    for slot in range(slots):
        total = total + image_length(groups[slot])
    return total


def row_places(groups, slots, first_row, count):
    rows = first_row + lax.broadcasted_iota(jnp.int32, (count, 1), 0)
    place = rows
    start = jnp.int32(0)
    for slot in range(slots):
        length = image_length(groups[slot])
        place = jnp.where((rows >= start) & (length > 0), rows - start, place)
        start = start + length
    live = rows < start
    prompt_slot = jnp.where(live & (place >= 1) & (place <= PROMPTS), place - 1, -1)
    return prompt_slot, live


def norm_parts(values):
    centered = values - jnp.mean(values, axis=-1, keepdims=True)
    rstd = lax.rsqrt(jnp.mean(centered * centered, axis=-1, keepdims=True) + EPSILON)
    return centered * rstd, rstd


def norm_back(normal, rstd, gain, grad):
    scaled = grad * gain
    return (
        scaled
        - jnp.mean(scaled, axis=-1, keepdims=True)
        - normal * jnp.mean(scaled * normal, axis=-1, keepdims=True)
    ) * rstd


def embed_kernel(
    slots, groups, tokens, pos_index, pos_table, prompts, gains, w_qkv, hidden_out, qkv_out, table
):
    tile = tokens.shape[0]
    step = pl.program_id(0)

    @pl.when(step == 0)
    def _():
        table[...] = jnp.zeros_like(table)
        table[: pos_table.shape[0]] = pos_table[...]
        rest = prompts[...]
        for piece in range(3):
            part = rest.astype(BF)
            first = POS_ROWS + piece * SLOT_ROWS
            table[first : first + PROMPTS] = part
            rest = rest - part.astype(F32)

    prompt_slot, _ = row_places(groups, slots, step * tile, tile)
    is_prompt = prompt_slot >= 0
    lane = lax.broadcasted_iota(jnp.int32, (1, POS_ROWS), 1)
    left = jnp.where(is_prompt, -1, pos_index[:, 0:1])
    right = jnp.where(is_prompt, -1, pos_index[:, 1:2])
    half_hot = jnp.where(lane == left, 0.5, 0.0) + jnp.where(lane == right, 0.5, 0.0)
    slot_lane = lax.broadcasted_iota(jnp.int32, (1, 3 * SLOT_ROWS), 1)
    slot_lane = lax.rem(slot_lane, SLOT_ROWS)
    slot_hot = jnp.where(slot_lane == prompt_slot, 1.0, 0.0)
    picked = dot(half_hot.astype(BF), table[:POS_ROWS]) + dot(
        slot_hot.astype(BF), table[POS_ROWS:]
    )
    hidden = jnp.where(is_prompt, 0.0, tokens[...].astype(F32)) + picked
    hidden_out[...] = hidden
    normal, _ = norm_parts(hidden)
    normed = (normal * gains[0:1]).astype(BF)
    qkv_out[...] = dot(normed, w_qkv[...]).astype(BF)


def embed(size_group, tokens, pos_index, pos_table, prompts, gains, w_qkv):
    rows, width = tokens.shape
    tile = 384
    keep = lambda i, g: (0, 0)
    whole = lambda a: pl.BlockSpec(a.shape, keep, pipeline_mode=pl.Buffered(1))
    by_row = lambda columns: pl.BlockSpec((tile, columns), lambda i, g: (i, 0))
    return pl.pallas_call(
        functools.partial(embed_kernel, size_group.shape[0]),
        grid_spec=pltpu.PrefetchScalarGridSpec(
            num_scalar_prefetch=1,
            grid=(rows // tile,),
            in_specs=[
                by_row(width),
                by_row(2),
                whole(pos_table),
                whole(prompts),
                whole(gains),
                whole(w_qkv),
            ],
            out_specs=[by_row(width), by_row(3 * width)],
            scratch_shapes=[pltpu.VMEM((POS_ROWS + 3 * SLOT_ROWS, width), BF)],
        ),
        out_shape=[
            jax.ShapeDtypeStruct((rows, width), F32),
            jax.ShapeDtypeStruct((rows, 3 * width), BF),
        ],
        compiler_params=pltpu.CompilerParams(vmem_limit_bytes=40 << 20),
        name="embed",
    )(size_group, tokens, pos_index, pos_table, prompts, gains, w_qkv)


def half(values, which):
    lane = lax.broadcasted_iota(jnp.int32, values.shape, 1)
    inside = (lane < HEAD_DIM) if which == 0 else (lane >= HEAD_DIM)
    return jnp.where(inside, values, jnp.zeros_like(values))


def each_image(groups, slots, image):
    def body(slot, start):
        group = groups[slot]
        length = image_length(group)
        pl.when(group == 2)(functools.partial(image, LARGE, start, length, slot))
        pl.when(group < 2)(functools.partial(image, SMALL, start, length, slot))
        return start + length

    lax.fori_loop(0, slots, body, jnp.int32(0))


def spread(pairs):
    for spaced, block in pairs:
        for pair in range(PAIRS):
            columns = slice(LANES * pair, LANES * (pair + 1))
            spaced[pair, : block.shape[0]] = block[:, columns].astype(F32)


def collect(block, spaced):
    for pair in range(PAIRS):
        columns = slice(LANES * pair, LANES * (pair + 1))
        block[:, columns] = spaced[pair, : block.shape[0]].astype(BF)


def take(spaced, rows):
    return [spaced[pair, rows, :] for pair in range(PAIRS)]


def low(parts):
    return [part.astype(BF) for part in parts]


def head_rows(parts, head):
    return parts[head // 2][HEAD_DIM * (head % 2) : HEAD_DIM * (head % 2 + 1)]


def clear_first(*refs):
    @pl.when(pl.program_id(0) == 0)
    def _():
        for ref in refs:
            ref[...] = jnp.zeros_like(ref)


def attend_kernel(slots, groups, q_ref, k_ref, v_ref, out_ref, total_ref, qs, ks, vs, outs):
    clear_first(qs, ks, vs, outs)
    spread(((qs, q_ref), (ks, k_ref), (vs, v_ref)))
    heads = range(GROUP_HEADS)

    def image(span, start, length, slot):
        rows = pl.ds(start, span)
        query = low(take(qs, rows))
        key = low(take(ks, rows))
        value_t = low([x.T for x in take(vs, rows)])
        last = span - LANES
        tail = lax.broadcasted_iota(jnp.int32, (LANES, 1), 0) + last < length
        for first, count in CHUNKS[span]:
            scores = [
                dot(key[h // 2], half(query[h // 2][first : first + count], h % 2), NT)
                for h in heads
            ]
            scores = [
                jnp.concatenate([s[:last], jnp.where(tail, s[last:], -1e30)], 0) for s in scores
            ]
            peaks = [jnp.max(s, axis=0, keepdims=True) for s in scores]
            powers = [jnp.exp2((s - m) * SCORE) for s, m in zip(scores, peaks)]
            totals = [jnp.sum(e, axis=0, keepdims=True) for e in powers]
            mixed = [dot(head_rows(value_t, h), powers[h].astype(BF)) for h in heads]
            mixed = [o / t for o, t in zip(mixed, totals)]
            for h in heads:
                total_ref[0, GROUP_HEADS * slot + h, :, first : first + count] = peaks[
                    h
                ] * SCORE + jnp.log2(totals[h])
            for pair in range(PAIRS):
                outs[pair, pl.ds(start + first, count), :] = jnp.concatenate(
                    mixed[2 * pair : 2 * pair + 2], 0
                ).T

    each_image(groups, slots, image)
    collect(out_ref, outs)


def attend(size_group, qkv):
    rows = qkv.shape[0]
    width = qkv.shape[1] // 3
    steps = width // HEAD_COLS
    slots = size_group.shape[0]
    block = lambda shift: pl.BlockSpec((rows, HEAD_COLS), lambda i, g: (0, shift * steps + i))
    spaced = pltpu.VMEM((PAIRS, rows + LANES, LANES), F32)
    return pl.pallas_call(
        functools.partial(attend_kernel, slots),
        grid_spec=pltpu.PrefetchScalarGridSpec(
            num_scalar_prefetch=1,
            grid=(steps,),
            in_specs=[block(0), block(1), block(2)],
            out_specs=[
                block(0),
                pl.BlockSpec((1, GROUP_HEADS * slots, 1, LARGE), lambda i, g: (i, 0, 0, 0)),
            ],
            scratch_shapes=[spaced] * 4,
        ),
        out_shape=[
            jax.ShapeDtypeStruct((rows, width), BF),
            jax.ShapeDtypeStruct((steps, GROUP_HEADS * slots, 1, LARGE), F32),
        ],
        compiler_params=pltpu.CompilerParams(vmem_limit_bytes=50 << 20),
        name="attend",
    )(size_group, qkv, qkv, qkv)


def attend_back_kernel(
    slots,
    groups,
    q_ref,
    k_ref,
    v_ref,
    grad_ref,
    mixed_ref,
    total_ref,
    dq_ref,
    dk_ref,
    dv_ref,
    qs,
    ks,
    vs,
    grads,
    mixes,
    dqs,
    dks,
    dvs,
):
    clear_first(qs, ks, vs, grads, mixes, dqs, dks, dvs)
    spread(((qs, q_ref), (ks, k_ref), (vs, v_ref), (grads, grad_ref), (mixes, mixed_ref)))
    heads = range(GROUP_HEADS)

    def image(span, start, length, slot):
        rows = pl.ds(start, span)
        query = low(take(qs, rows))
        key = low(take(ks, rows))
        key_t = low([x.T for x in take(ks, rows)])
        value = low(take(vs, rows))
        inside = lax.broadcasted_iota(jnp.int32, (span, 1), 0) < length
        grad32 = [jnp.where(inside, x, 0.0) for x in take(grads, rows)]
        products = [(x * y).T for x, y in zip(grad32, take(mixes, rows))]
        grad = low(grad32)
        last = span - LANES
        tail = inside[last:]
        dk = [jnp.zeros((span, LANES), F32)] * PAIRS
        dv = [jnp.zeros((span, LANES), F32)] * PAIRS
        for first, count in CHUNKS[span]:
            part = slice(first, first + count)
            query_h = [half(query[h // 2][part], h % 2) for h in heads]
            grad_h = [half(grad[h // 2][part], h % 2) for h in heads]
            scores = [dot(key[h // 2], query_h[h], NT) for h in heads]
            prob_grads = [dot(value[h // 2], grad_h[h], NT) for h in heads]
            probs = [
                jnp.exp2(scores[h] * SCORE - total_ref[0, GROUP_HEADS * slot + h, :, part])
                for h in heads
            ]
            probs = [
                jnp.concatenate([p[:last], jnp.where(tail, p[last:], 0.0)], 0) for p in probs
            ]
            deltas = [
                jnp.sum(head_rows(products, h)[:, part], axis=0, keepdims=True) for h in heads
            ]
            score_grads = [(probs[h] * (prob_grads[h] - deltas[h])).astype(BF) for h in heads]
            for h in heads:
                dv[h // 2] += dot(probs[h].astype(BF), grad_h[h])
                dk[h // 2] += dot(score_grads[h], query_h[h])
            dq = [dot(head_rows(key_t, h), score_grads[h]) for h in heads]
            for pair in range(PAIRS):
                dqs[pair, pl.ds(start + first, count), :] = (
                    jnp.concatenate(dq[2 * pair : 2 * pair + 2], 0).T * SCALE
                )
        for pair in range(PAIRS):
            dks[pair, rows, :] = dk[pair] * SCALE
            dvs[pair, rows, :] = dv[pair]

    each_image(groups, slots, image)
    collect(dq_ref, dqs)
    collect(dk_ref, dks)
    collect(dv_ref, dvs)


def attend_back(size_group, qkv, mixed_grad, mixed, totals):
    rows = qkv.shape[0]
    width = qkv.shape[1] // 3
    steps = width // HEAD_COLS
    slots = size_group.shape[0]
    block = lambda shift: pl.BlockSpec((rows, HEAD_COLS), lambda i, g: (0, shift * steps + i))
    spaced = pltpu.VMEM((PAIRS, rows + LANES, LANES), F32)
    return pl.pallas_call(
        functools.partial(attend_back_kernel, slots),
        grid_spec=pltpu.PrefetchScalarGridSpec(
            num_scalar_prefetch=1,
            grid=(steps,),
            in_specs=[
                block(0),
                block(1),
                block(2),
                block(0),
                block(0),
                pl.BlockSpec((1, GROUP_HEADS * slots, 1, LARGE), lambda i, g: (i, 0, 0, 0)),
            ],
            out_specs=[block(0)] * 3,
            scratch_shapes=[spaced] * 8,
        ),
        out_shape=[jax.ShapeDtypeStruct((rows, width), BF)] * 3,
        compiler_params=pltpu.CompilerParams(vmem_limit_bytes=56 << 20),
        name="attend_back",
    )(size_group, qkv, qkv, qkv, mixed_grad, mixed, totals)


def feed_kernel(
    slots,
    chunk,
    groups,
    hidden,
    mixed,
    cotangent,
    gains,
    w_out,
    w_up,
    w_down,
    out_ref,
    middle_grad_ref,
    mixed_grad_ref,
):
    tile = hidden.shape[0]
    inner_width = w_up.shape[1]
    rows = pl.program_id(0) * tile + lax.broadcasted_iota(jnp.int32, (tile, 1), 0)
    live = rows < total_length(groups, slots)
    out_grad = jnp.where(live, cotangent[...].astype(F32), 0.0)
    out_grad_low = out_grad.astype(BF)
    middle = hidden[...] + dot(mixed[...], w_out[...])
    normal, rstd = norm_parts(middle)
    gain = gains[1:2]
    second = (normal * gain).astype(BF)
    forward = middle
    back = jnp.zeros_like(middle)
    for first in range(0, inner_width, chunk):
        part = slice(first, first + chunk)
        inner = dot(second, w_up[:, part])
        act_grad = dot(out_grad_low, w_down[part], NT)
        phi = 0.5 + 0.5 * lax.erf(inner * (0.5**0.5))
        density = jnp.exp2(inner * inner * (-0.5 * LOG2E)) * 0.3989422804014327
        activated = (inner * phi).astype(BF)
        inner_grad = (act_grad * (phi + inner * density)).astype(BF)
        forward = forward + dot(activated, w_down[part])
        back = back + dot(inner_grad, w_up[:, part], NT)
    out_ref[...] = jnp.where(live, forward, 0.0).astype(BF)
    middle_grad = out_grad + norm_back(normal, rstd, gain, back)
    middle_grad_ref[...] = middle_grad
    mixed_grad_ref[...] = dot(middle_grad.astype(BF), w_out[...], NT).astype(BF)


def feed(size_group, hidden, mixed, cotangent, gains, w_out, w_up, w_down):
    rows, width = hidden.shape
    tile = 384
    chunk = 512
    keep = lambda i, g: (0, 0)
    whole = lambda a: pl.BlockSpec(a.shape, keep, pipeline_mode=pl.Buffered(1))
    by_row = pl.BlockSpec((tile, width), lambda i, g: (i, 0))
    return pl.pallas_call(
        functools.partial(feed_kernel, size_group.shape[0], chunk),
        grid_spec=pltpu.PrefetchScalarGridSpec(
            num_scalar_prefetch=1,
            grid=(rows // tile,),
            in_specs=[by_row, by_row, by_row, whole(gains), whole(w_out), whole(w_up), whole(w_down)],
            out_specs=[by_row, by_row, by_row],
        ),
        out_shape=[
            jax.ShapeDtypeStruct((rows, width), BF),
            jax.ShapeDtypeStruct((rows, width), F32),
            jax.ShapeDtypeStruct((rows, width), BF),
        ],
        compiler_params=pltpu.CompilerParams(vmem_limit_bytes=56 << 20),
        name="feed",
    )(size_group, hidden, mixed, cotangent, gains, w_out, w_up, w_down)


def finish_kernel(
    slots, groups, hidden, middle_grad, dq, dk, dv, gains, w_qkv, grad_ref, sums_ref, kept
):
    tile, width = hidden.shape
    step = pl.program_id(0)
    normed_grad = (
        dot(dq[...], w_qkv[:, :width], NT)
        + dot(dk[...], w_qkv[:, width : 2 * width], NT)
        + dot(dv[...], w_qkv[:, 2 * width :], NT)
    )
    normal, rstd = norm_parts(hidden[...])
    hidden_grad = middle_grad[...] + norm_back(normal, rstd, gains[0:1], normed_grad)
    prompt_slot, live = row_places(groups, slots, step * tile, tile)
    grad_ref[...] = jnp.where(live & (prompt_slot < 0), hidden_grad, 0.0).astype(BF)
    for column in range(width // LANES):
        kept[column, pl.ds(pl.multiple_of(step * tile, tile), tile), :] = hidden_grad[
            :, LANES * column : LANES * (column + 1)
        ]

    @pl.when(step == pl.num_programs(0) - 1)
    def _():
        total = total_length(groups, slots).astype(F32)
        slot_row = lax.broadcasted_iota(jnp.int32, (SLOT_ROWS, LANES), 0)
        for column in range(width // LANES):
            start = jnp.int32(0)
            sums = jnp.zeros((SLOT_ROWS, LANES), F32)
            for slot in range(slots):
                length = image_length(groups[slot])
                first = jnp.where(length > 0, start + 1, 0)
                taken = kept[column, pl.ds(first, SLOT_ROWS), :]
                sums = sums + jnp.where(length > 0, taken, 0.0)
                start = start + length
            sums_ref[:, LANES * column : LANES * (column + 1)] = jnp.where(
                slot_row < PROMPTS, sums, jnp.where(slot_row == PROMPTS, total, 0.0)
            )


def finish(size_group, hidden, middle_grad, dq, dk, dv, gains, w_qkv):
    rows, width = hidden.shape
    tile = 384
    keep = lambda i, g: (0, 0)
    whole = lambda a: pl.BlockSpec(a.shape, keep, pipeline_mode=pl.Buffered(1))
    by_row = pl.BlockSpec((tile, width), lambda i, g: (i, 0))
    return pl.pallas_call(
        functools.partial(finish_kernel, size_group.shape[0]),
        grid_spec=pltpu.PrefetchScalarGridSpec(
            num_scalar_prefetch=1,
            grid=(rows // tile,),
            in_specs=[by_row] * 5 + [whole(gains), whole(w_qkv)],
            out_specs=[by_row, pl.BlockSpec((SLOT_ROWS, width), keep)],
            scratch_shapes=[pltpu.VMEM((width // LANES, rows, LANES), F32)],
        ),
        out_shape=[
            jax.ShapeDtypeStruct((rows, width), BF),
            jax.ShapeDtypeStruct((SLOT_ROWS, width), F32),
        ],
        compiler_params=pltpu.CompilerParams(vmem_limit_bytes=50 << 20),
        name="finish",
    )(size_group, hidden, middle_grad, dq, dk, dv, gains, w_qkv)


def shards(
    axes,
    tokens,
    pos_index,
    size_group,
    pos_table,
    prompts,
    norm_gains,
    w_qkv,
    w_out,
    w_up,
    w_down,
    cotangent,
):
    full_qkv = lax.all_gather(w_qkv, "wide", axis=0, tiled=True)
    full_out = lax.all_gather(w_out, "wide", axis=0, tiled=True)
    full_up = lax.all_gather(w_up, "wide", axis=0, tiled=True)
    full_down = lax.all_gather(w_down, "wide", axis=0, tiled=True)
    hidden, qkv = embed(size_group, tokens, pos_index, pos_table, prompts, norm_gains, full_qkv)
    mixed, totals = attend(size_group, qkv)
    outputs, middle_grad, mixed_grad = feed(
        size_group, hidden, mixed, cotangent, norm_gains, full_out, full_up, full_down
    )
    dq, dk, dv = attend_back(size_group, qkv, mixed_grad, mixed, totals)
    input_grad, sums = finish(size_group, hidden, middle_grad, dq, dk, dv, norm_gains, full_qkv)
    sums = lax.psum(sums, ("dp", "wide"))
    token_total = sums[PROMPTS, 0]
    prompt_grad = sums[:PROMPTS] + (2.0 * PENALTY_RATE / prompts.size) * token_total * prompts
    penalty = PENALTY_RATE * token_total * jnp.mean(prompts * prompts)
    return (outputs, input_grad, prompt_grad, penalty)


def solution(mesh):
    return jax.shard_map(
        functools.partial(shards, tuple(mesh.shape.items())),
        mesh=mesh,
        in_specs=(
            P(("dp", "wide"), None),
            P(("dp", "wide"), None),
            P(("dp", "wide")),
            P(),
            P(),
            P(),
            P("wide", None),
            P("wide", None),
            P("wide", None),
            P("wide", None),
            P(("dp", "wide"), None),
        ),
        out_specs=(P(("dp", "wide"), None), P(("dp", "wide"), None), P(), P()),
        check_vma=False,
    )
```

time: 711 us -> 395 us (0.56); the launches traced: 702 us -> 395 us
  matrix products: 306 us -> 0 us
  waiting for transfers between devices: 101 us -> 290 us
  blocking collectives: 86.2 us -> 0 us
  other arithmetic: 80.1 us -> 2.23 us
  Pallas kernels: 0 us -> 75 us
  local copies, waits for them, and re-layouts: 81.7 us -> 10.1 us
  loops' own time: 28.3 us -> 0 us
    dot_general x29 -> x0, matrix products: 306 us -> none  [the longest x3 51.9 us: attend_back(): jnp.einsum('hqd,hkd->hqk', head_grad, value_rows, preferred_element_type=...]
    all_gather x4, waiting for transfers between devices: 0.04 us -> 150 us  [the longest x1 53.2 us: shards(): full_up = lax.all_gather(w_up, 'wide', axis=0, tiled=True)]
    psum x0 -> x1, waiting for transfers between devices: none -> 138 us  [shards(): sums = lax.psum(sums, ('dp', 'wide'))]
    unnamed x6 -> x5, waiting for transfers between devices: 101 us -> 2.6 us
    pallas_call x0 -> x5, Pallas kernels: none -> 75 us  [the longest x1 36.6 us: feed(): pl.pallas_call(functools.partial(feed_kernel, size_group.shape[0], chunk)...]
    convert_element_type x5 -> x0, other arithmetic: 45.5 us -> none  [the longest x3 41.7 us: attend_back(): score_grad = (attn_probs * (prob_grad - jnp.sum(prob_grad * attn_probs, a...]
    all_gather x1 -> x0, blocking collectives: 44 us -> none  [shards(): lax.all_gather(share + pen_rate * own_prompts, ('dp', 'wide'), axis=1, ti...]
    psum x1 -> x0, blocking collectives: 42.2 us -> none  [shards(): token_total = lax.psum(count_local, ('dp', 'wide'))]
  transfers between devices with their start and end apart: 5 -> 5, of which waited for: 1 -> 5; matrix products, arithmetic and copies ran while one was open for 25% -> 0% of each run, Pallas kernels for 0% -> 4%
where the time goes in v1:
time: 395 us
  waiting for transfers between devices  290 us (73%)
  Pallas kernels  75 us (19%)
  between operations  17 us (4%)
  local copies, waits for them, and re-layouts  10.1 us (3%)
    psum x1, waiting for transfers between devices, shards(): sums = lax.psum(sums, ('dp', 'wide'))  138 us
    all_gather x1, waiting for transfers between devices, shards(): full_up = lax.all_gather(w_up, 'wide', axis=0, tiled=True)  53.2 us
    all_gather x1, waiting for transfers between devices, shards(): full_down = lax.all_gather(w_down, 'wide', axis=0, tiled=True)  52 us
    all_gather x1, waiting for transfers between devices, shards(): full_qkv = lax.all_gather(w_qkv, 'wide', axis=0, tiled=True)  43.6 us
    pallas_call x1, Pallas kernels, feed(): pl.pallas_call(functools.partial(feed_kernel, size_group.shape[0], chunk)...  36.6 us
    pallas_call x1, Pallas kernels, finish(): pl.pallas_call(functools.partial(finish_kernel, size_group.shape[0]), gri...  12 us
    pallas_call x1, Pallas kernels, attend_back(): pl.pallas_call(functools.partial(attend_back_kernel, slots), grid_spec=pl...  10.5 us
    pallas_call x1, Pallas kernels, embed(): pl.pallas_call(functools.partial(embed_kernel, size_group.shape[0]), grid...  9.81 us
  transfers between devices with their start and end apart: 5, of which 5 were waited for; matrix products, arithmetic and copies ran while one was open for 0% of the time, Pallas kernels for 4%

profile of v1, /device:TPU:0, one launch (start us, length us, event | category | flops | bytes accessed | tf_op | source)
XLA Modules:
  0.0 395.0 jit_solution(5472252098663273743)
XLA Ops:
  7.3 0.7 all-gather.5.cloned.1.call-update
  8.0 0.7 all-gather.7.cloned.1.call-update
  8.8 0.7 all-gather.9.cloned.1.call-update
  9.5 0.5 all-gather.11.cloned.1.call-update
  10.0 0.0 all-reduce.2.cloned.1.call-start
  10.1 0.2 copy.15.pos_index
  10.3 43.6 %all-gather.5.cloned.1.call-done.w_qkv = bf16[768,2304]{1,0:T(8,128)(2,1)} async-done(((bf16[96,2304]{1,0:T(8,128)(2,1)}), bf16[768,2304]{1,0:T(8,128)(2,1)}) %all-gather.5.cloned.1.call-update) | async-done | bytes 3538960 | tf_op jit(solution)/shard_map/all_gather | solution.py:512
  54.0 2.0 copy-done
  56.0 9.8 %embed.1 = (f32[1152,768]{1,0:T(8,128)S(1)}, bf16[1152,2304]{1,0:T(8,128)(2,1)}) custom-call(s32[7]{0:T(128)S(1)} %copy-done.11, bf16[1152,768]{1,0:T(8,128)(2,1)S(1)} %copy-done.3, s32[1152,2]{1,0:T(8,128)S(1)} %copy.15.pos_index, bf16[197,768]{1,0:T(8,128)(2,1)S(1)} %copy-done.7, f32[50,768]{1,0:T(8,128)S(1)} %copy-done.6, f32[2,768]{1,0:T(2,128)S(1)} %copy-done.9, ...), custom_call_target="tpu_custom_call" | custom-call | tf_op jit(solution)/shard_map/embed/pallas_call | solution.py:126
  65.8 1.8 copy-done.1
  67.6 6.2 %attend.1 = (bf16[1152,768]{1,0:T(8,128)(2,1)S(1)}, f32[3,28,1,640]{3,2,1,0:T(1,128)S(1)}) custom-call(s32[7]{0:T(128)S(1)} %copy-done.11, bf16[1152,2304]{1,0:T(8,128)(2,1)} %get-tuple-element.17.q_ref.k_ref.v_ref, bf16[1152,2304]{1,0:T(8,128)(2,1)} %get-tuple-element.17.q_ref.k_ref.v_ref, bf16[1152,2304]{1,0:T(8,128)(2,1)} %get-tuple-element.17.q_ref.k_ref.v_ref), custom_call_target="tpu_custom_call" | custom-call | tf_op jit(solution)/shard_map/attend/pallas_call | solution.py:245
  73.8 1.2 copy-done.2
  75.0 0.7 copy-done.8
  75.7 1.5 all-gather.7.cloned.1.call-done.w_out
  77.2 53.2 %all-gather.9.cloned.1.call-done.w_up = bf16[768,3072]{1,0:T(8,128)(2,1)} async-done(((bf16[96,3072]{1,0:T(8,128)(2,1)}), bf16[768,3072]{1,0:T(8,128)(2,1)}) %all-gather.9.cloned.1.call-update) | async-done | bytes 4718608 | tf_op jit(solution)/shard_map/all_gather | solution.py:514
  130.3 52.0 %all-gather.11.cloned.1.call-done.w_down = bf16[3072,768]{1,0:T(8,128)(2,1)} async-done(((bf16[384,768]{1,0:T(8,128)(2,1)}), bf16[3072,768]{1,0:T(8,128)(2,1)}) %all-gather.11.cloned.1.call-update) | async-done | bytes 4718608 | tf_op jit(solution)/shard_map/all_gather | solution.py:515
  182.4 36.6 %feed.1 = (bf16[1152,768]{1,0:T(8,128)(2,1)}, f32[1152,768]{1,0:T(8,128)}, bf16[1152,768]{1,0:T(8,128)(2,1)}) custom-call(s32[7]{0:T(128)} %groups.9, f32[1152,768]{1,0:T(8,128)} %copy-done.1, bf16[1152,768]{1,0:T(8,128)(2,1)} %copy-done.2, bf16[1152,768]{1,0:T(8,128)(2,1)} %cotangent.1, f32[2,768]{1,0:T(2,128)} %gains.5, ...), custom_call_target="tpu_custom_call" | custom-call | tf_op jit(solution)/shard_map/feed/pallas_call | solution.py:419
  219.0 10.5 %attend_back.1 = (bf16[1152,768]{1,0:T(8,128)(2,1)}, bf16[1152,768]{1,0:T(8,128)(2,1)}, bf16[1152,768]{1,0:T(8,128)(2,1)}) custom-call(s32[7]{0:T(128)} %groups.9, bf16[1152,2304]{1,0:T(8,128)(2,1)} %get-tuple-element.17.q_ref.k_ref.v_ref, bf16[1152,2304]{1,0:T(8,128)(2,1)} %get-tuple-element.17.q_ref.k_ref.v_ref, ...), custom_call_target="tpu_custom_call" | custom-call | tf_op jit(solution)/shard_map/attend_back/pallas_call | solution.py:347
  229.4 1.5 copy-done.4
  230.9 1.5 copy-done.5
  232.4 12.0 %finish.1 = (bf16[1152,768]{1,0:T(8,128)(2,1)}, f32[64,768]{1,0:T(8,128)}) custom-call(s32[7]{0:T(128)S(1)} %copy-done.12, f32[1152,768]{1,0:T(8,128)} %copy-done.1, f32[1152,768]{1,0:T(8,128)} %get-tuple-element.20.middle_grad, bf16[1152,768]{1,0:T(8,128)(2,1)S(1)} %copy-done.4, bf16[1152,768]{1,0:T(8,128)(2,1)S(1)} %copy-done.5, ...), custom_call_target="tpu_custom_call" | custom-call | tf_op jit(solution)/shard_map/finish/pallas_call | solution.py:480
  244.4 137.6 %all-reduce.2.cloned.1.call-done = f32[64,768]{1,0:T(8,128)} async-done(((f32[64,768]{1,0:T(8,128)}), f32[64,768]{1,0:T(8,128)}) %all-reduce.2.cloned.1.call-update) | async-done | bytes 196624 | tf_op jit(solution)/shard_map/psum | solution.py:523
  382.0 1.2 slice.9
  383.8 2.2 multiply_reduce_fusion
  (27 shorter events, 0.2 us)
Async XLA Ops:
  7.2 2.9 copy-start.13
  7.2 46.8 %copy-start.11 = (s32[7]{0:T(128)S(1)}, s32[7]{0:T(128)}, u32[]{:S(2)}) copy-start(s32[7]{0:T(128)} %groups.9) | copy-start | bytes 88
  7.2 46.8 %copy-start.9 = (f32[2,768]{1,0:T(2,128)S(1)}, f32[2,768]{1,0:T(2,128)}, u32[]{:S(2)}) copy-start(f32[2,768]{1,0:T(2,128)} %gains.5) | copy-start | bytes 18436
  7.2 46.8 %copy-start.6 = (f32[50,768]{1,0:T(8,128)S(1)}, f32[50,768]{1,0:T(8,128)}, u32[]{:S(2)}) copy-start(f32[50,768]{1,0:T(8,128)} %prompts.1) | copy-start | bytes 460804
  7.2 46.8 %copy-start.7 = (bf16[197,768]{1,0:T(8,128)(2,1)S(1)}, bf16[197,768]{1,0:T(8,128)(2,1)}, u32[]{:S(2)}) copy-start(bf16[197,768]{1,0:T(8,128)(2,1)} %pos_table.1) | copy-start | bytes 907780
  7.2 46.8 %copy-start.3 = (bf16[1152,768]{1,0:T(8,128)(2,1)S(1)}, bf16[1152,768]{1,0:T(8,128)(2,1)}, u32[]{:S(2)}) copy-start(bf16[1152,768]{1,0:T(8,128)(2,1)} %tokens.1) | copy-start | bytes 5308420
  7.2 46.7 %all-gather.5.cloned.1.call-start = ((), (), s32[]{:S(2)}) async-start(), calls=%async_computation | async-start | bytes 3981312 | tf_op jit(solution)/shard_map/all_gather | solution.py:512
  8.0 69.2 %all-gather.7.cloned.1.call-start = ((), (), s32[]{:S(2)}) async-start(), calls=%async_computation.1 | async-start | bytes 1327104 | tf_op jit(solution)/shard_map/all_gather | solution.py:513
  8.7 121.6 %all-gather.9.cloned.1.call-start = ((), (), s32[]{:S(2)}) async-start(), calls=%async_computation.2 | async-start | bytes 5308416 | tf_op jit(solution)/shard_map/all_gather | solution.py:514
  9.4 172.9 %all-gather.11.cloned.1.call-start = ((), (), s32[]{:S(2)}) async-start(), calls=%async_computation.3 | async-start | bytes 5308416 | tf_op jit(solution)/shard_map/all_gather | solution.py:515
  10.0 371.9 %all-reduce.2.cloned.1.call-start = ((), (), s32[]{:S(2)}) async-start(), calls=%async_computation.4 | async-start | bytes 393216 | tf_op jit(solution)/shard_map/psum | solution.py:523
  54.0 2.0 copy-start
  65.8 1.8 copy-start.1
  73.8 1.2 copy-start.2
  75.0 0.7 copy-start.8
  219.0 10.5 %copy-start.10 = (f32[2,768]{1,0:T(2,128)S(1)}, f32[2,768]{1,0:T(2,128)}, u32[]{:S(2)}) copy-start(f32[2,768]{1,0:T(2,128)} %gains.5) | copy-start | bytes 18436
  219.0 10.5 %copy-start.12 = (s32[7]{0:T(128)S(1)}, s32[7]{0:T(128)}, u32[]{:S(2)}) copy-start(s32[7]{0:T(128)} %groups.9) | copy-start | bytes 88
  229.4 1.5 copy-start.4
  230.9 1.5 copy-start.5
Sparse Core Ops, SparseCore 0:
  9.7 44.2 all-gather.4
  55.6 21.5 all-gather.6
  78.8 51.4 all-gather.8
  131.8 50.5 all-gather.10
  244.5 137.4 all-reduce.1

commit v2 on v1

--- a/solution.py
+++ b/solution.py
@@ -495,6 +495,130 @@
     )(size_group, hidden, middle_grad, dq, dk, dv, gains, w_qkv)
 
 
+def share_kernel(
+    dp, wide, sums, prompts, grad_ref, penalty_ref, near, far, result, send, near_in, far_in, last_in
+):
+    members = 2 * dp
+    planes = wide // 2
+    slice_rows = SLOT_ROWS // members
+    d = lax.axis_index("dp")
+    w = lax.axis_index("wide")
+    plane = w // 2
+    member = d * 2 + lax.rem(w, 2)
+
+    def peer(step):
+        other = lax.rem(member + step, members)
+        return other, (other // 2, plane * 2 + lax.rem(other, 2))
+
+    def plane_peer(step):
+        other = lax.rem(plane + step, planes)
+        return other, (d, other * 2 + lax.rem(w, 2))
+
+    barrier = pltpu.get_barrier_semaphore()
+    for step in range(1, members):
+        pl.semaphore_signal(barrier, inc=1, device_id=peer(step)[1], device_id_type=MESH)
+    for step in range(1, planes):
+        pl.semaphore_signal(barrier, inc=1, device_id=plane_peer(step)[1], device_id_type=MESH)
+    pl.semaphore_wait(barrier, members + planes - 2)
+
+    def part(ref, index):
+        return ref.at[pl.ds(pl.multiple_of(index * slice_rows, slice_rows), slice_rows)]
+
+    first = []
+    for step in range(1, members):
+        other, device = peer(step)
+        first.append(
+            pltpu.make_async_remote_copy(
+                part(sums, other),
+                near.at[step],
+                send.at[0, step],
+                near_in.at[step],
+                device_id=device,
+                device_id_type=MESH,
+            )
+        )
+        first[-1].start()
+    near[0] = part(sums, member)[...]
+    for copy in first:
+        copy.wait_recv()
+    total = jnp.zeros(near.shape[1:], F32)
+    for index in range(members):
+        total = total + near[lax.rem(member - index + members, members)]
+    far[plane] = total
+    second = []
+    for step in range(1, planes):
+        other, device = plane_peer(step)
+        second.append(
+            pltpu.make_async_remote_copy(
+                far.at[plane],
+                far.at[plane],
+                send.at[1, step],
+                far_in.at[step],
+                device_id=device,
+                device_id_type=MESH,
+            )
+        )
+        second[-1].start()
+    for copy in second:
+        copy.wait_recv()
+    total = jnp.zeros(near.shape[1:], F32)
+    for index in range(planes):
+        total = total + far[index]
+    part(result, member)[...] = total
+    third = []
+    for step in range(1, members):
+        other, device = peer(step)
+        third.append(
+            pltpu.make_async_remote_copy(
+                part(result, member),
+                part(result, member),
+                send.at[2, step],
+                last_in.at[step],
+                device_id=device,
+                device_id_type=MESH,
+            )
+        )
+        third[-1].start()
+    for copy in third:
+        copy.wait_recv()
+    for copy in first + second + third:
+        copy.wait_send()
+    known = prompts[...]
+    count = result[PROMPTS : PROMPTS + 1]
+    size = known.shape[0] * known.shape[1]
+    grad_ref[...] = result[:PROMPTS] + (2.0 * PENALTY_RATE / size) * count * known
+    square = jnp.sum(jnp.sum(known * known, axis=1, keepdims=True), axis=0, keepdims=True)
+    penalty_ref[...] = PENALTY_RATE * count[:, :1] * (square / size)
+
+
+def share(axes, sums, prompts):
+    dp, wide = axes["dp"], axes["wide"]
+    members, planes = 2 * dp, wide // 2
+    rows, width = sums.shape
+    dma = pltpu.SemaphoreType.DMA
+    grad, penalty = pl.pallas_call(
+        functools.partial(share_kernel, dp, wide),
+        in_specs=[pl.BlockSpec(memory_space=pltpu.VMEM)] * 2,
+        out_specs=[pl.BlockSpec(memory_space=pltpu.VMEM)] * 2,
+        out_shape=[
+            jax.ShapeDtypeStruct(prompts.shape, F32),
+            jax.ShapeDtypeStruct((1, 1), F32),
+        ],
+        scratch_shapes=[
+            pltpu.VMEM((members, rows // members, width), F32),
+            pltpu.VMEM((planes, rows // members, width), F32),
+            pltpu.VMEM((rows, width), F32),
+            dma((3, max(members, planes))),
+            dma((members,)),
+            dma((planes,)),
+            dma((members,)),
+        ],
+        compiler_params=pltpu.CompilerParams(collective_id=1, has_side_effects=True),
+        name="share",
+    )(sums, prompts)
+    return grad, penalty[0, 0]
+
+
 def shards(
     axes,
     tokens,
@@ -520,16 +644,13 @@
     )
     dq, dk, dv = attend_back(size_group, qkv, mixed_grad, mixed, totals)
     input_grad, sums = finish(size_group, hidden, middle_grad, dq, dk, dv, norm_gains, full_qkv)
-    sums = lax.psum(sums, ("dp", "wide"))
-    token_total = sums[PROMPTS, 0]
-    prompt_grad = sums[:PROMPTS] + (2.0 * PENALTY_RATE / prompts.size) * token_total * prompts
-    penalty = PENALTY_RATE * token_total * jnp.mean(prompts * prompts)
+    prompt_grad, penalty = share(axes, sums, prompts)
     return (outputs, input_grad, prompt_grad, penalty)
 
 
 def solution(mesh):
     return jax.shard_map(
-        functools.partial(shards, tuple(mesh.shape.items())),
+        functools.partial(shards, dict(mesh.shape)),
         mesh=mesh,
         in_specs=(
             P(("dp", "wide"), None),

time: 395 us -> 287 us (0.73)
  waiting for transfers between devices: 290 us -> 153 us
  Pallas kernels: 75 us -> 106 us
    psum x1 -> x0, waiting for transfers between devices: 138 us -> none  [shards(): sums = lax.psum(sums, ('dp', 'wide'))]
    pallas_call x0 -> x1, Pallas kernels: none -> 31.5 us  [share(): pl.pallas_call(functools.partial(share_kernel, dp, wide), in_specs=[pl.Bl...]
    unnamed x29 -> x32, local copies, waits for them, and re-layouts: 8.89 us -> 11.2 us
  transfers between devices with their start and end apart: 5 -> 4, of which waited for: 5 -> 4; matrix products, arithmetic and copies ran while one was open for 0% -> 0% of each run, Pallas kernels for 4% -> 6%
where the time goes in v2:
time: 287 us; the launch traced here: 286 us
  waiting for transfers between devices  153 us (53%)
  Pallas kernels  106 us (37%)
  between operations  15.6 us (5%)
  local copies, waits for them, and re-layouts  11.2 us (4%)
    all_gather x1, waiting for transfers between devices, shards(): full_up = lax.all_gather(w_up, 'wide', axis=0, tiled=True)  53.1 us
    all_gather x1, waiting for transfers between devices, shards(): full_down = lax.all_gather(w_down, 'wide', axis=0, tiled=True)  52 us
    all_gather x1, waiting for transfers between devices, shards(): full_qkv = lax.all_gather(w_qkv, 'wide', axis=0, tiled=True)  43.7 us
    pallas_call x1, Pallas kernels, feed(): pl.pallas_call(functools.partial(feed_kernel, size_group.shape[0], chunk)...  36.6 us
    pallas_call x1, Pallas kernels, share(): pl.pallas_call(functools.partial(share_kernel, dp, wide), in_specs=[pl.Bl...  31.5 us
    pallas_call x1, Pallas kernels, finish(): pl.pallas_call(functools.partial(finish_kernel, size_group.shape[0]), gri...  11.9 us
    unnamed x32, local copies, waits for them, and re-layouts  11.2 us
    pallas_call x1, Pallas kernels, attend_back(): pl.pallas_call(functools.partial(attend_back_kernel, slots), grid_spec=pl...  10.4 us
  transfers between devices with their start and end apart: 4, of which 4 were waited for; matrix products, arithmetic and copies ran while one was open for 0% of the time, Pallas kernels for 6%

profile of v2, /device:TPU:0, one launch (start us, length us, event | category | flops | bytes accessed | tf_op | source)
XLA Modules:
  0.0 286.3 jit_solution(7620680515794651193)
XLA Ops:
  7.3 0.7 all-gather.5.cloned.1.call-update
  8.0 0.7 all-gather.7.cloned.1.call-update
  8.8 0.7 all-gather.9.cloned.1.call-update
  9.4 0.0 all-gather.11.cloned.1.call-start
  9.5 0.5 all-gather.11.cloned.1.call-update
  10.0 0.2 copy.15.pos_index
  10.3 43.7 %all-gather.5.cloned.1.call-done.w_qkv = bf16[768,2304]{1,0:T(8,128)(2,1)} async-done(((bf16[96,2304]{1,0:T(8,128)(2,1)}), bf16[768,2304]{1,0:T(8,128)(2,1)}) %all-gather.5.cloned.1.call-update) | async-done | bytes 3538960 | tf_op jit(solution)/shard_map/all_gather | solution.py:636
  54.0 2.0 copy-done
  56.0 9.7 %embed.1 = (f32[1152,768]{1,0:T(8,128)S(1)}, bf16[1152,2304]{1,0:T(8,128)(2,1)}) custom-call(s32[7]{0:T(128)S(1)} %copy-done.12, bf16[1152,768]{1,0:T(8,128)(2,1)S(1)} %copy-done.3, s32[1152,2]{1,0:T(8,128)S(1)} %copy.15.pos_index, bf16[197,768]{1,0:T(8,128)(2,1)S(1)} %copy-done.7, f32[50,768]{1,0:T(8,128)S(1)} %copy-done.6, f32[2,768]{1,0:T(2,128)S(1)} %copy-done.10, ...), custom_call_target="tpu_custom_call" | custom-call | tf_op jit(solution)/shard_map/embed/pallas_call | solution.py:126
  65.6 1.8 copy-done.1
  67.5 6.2 %attend.1 = (bf16[1152,768]{1,0:T(8,128)(2,1)S(1)}, f32[3,28,1,640]{3,2,1,0:T(1,128)S(1)}) custom-call(s32[7]{0:T(128)S(1)} %copy-done.12, bf16[1152,2304]{1,0:T(8,128)(2,1)} %get-tuple-element.19.q_ref.k_ref.v_ref, bf16[1152,2304]{1,0:T(8,128)(2,1)} %get-tuple-element.19.q_ref.k_ref.v_ref, bf16[1152,2304]{1,0:T(8,128)(2,1)} %get-tuple-element.19.q_ref.k_ref.v_ref), custom_call_target="tpu_custom_call" | custom-call | tf_op jit(solution)/shard_map/attend/pallas_call | solution.py:245
  73.7 1.2 copy-done.2
  74.9 0.7 copy-done.8
  75.6 1.6 all-gather.7.cloned.1.call-done.w_out
  77.2 53.1 %all-gather.9.cloned.1.call-done.w_up = bf16[768,3072]{1,0:T(8,128)(2,1)} async-done(((bf16[96,3072]{1,0:T(8,128)(2,1)}), bf16[768,3072]{1,0:T(8,128)(2,1)}) %all-gather.9.cloned.1.call-update) | async-done | bytes 4718608 | tf_op jit(solution)/shard_map/all_gather | solution.py:638
  130.3 52.0 %all-gather.11.cloned.1.call-done.w_down = bf16[3072,768]{1,0:T(8,128)(2,1)} async-done(((bf16[384,768]{1,0:T(8,128)(2,1)}), bf16[3072,768]{1,0:T(8,128)(2,1)}) %all-gather.11.cloned.1.call-update) | async-done | bytes 4718608 | tf_op jit(solution)/shard_map/all_gather | solution.py:639
  182.4 36.6 %feed.1 = (bf16[1152,768]{1,0:T(8,128)(2,1)}, f32[1152,768]{1,0:T(8,128)}, bf16[1152,768]{1,0:T(8,128)(2,1)}) custom-call(s32[7]{0:T(128)} %groups.9, f32[1152,768]{1,0:T(8,128)} %copy-done.1, bf16[1152,768]{1,0:T(8,128)(2,1)} %copy-done.2, bf16[1152,768]{1,0:T(8,128)(2,1)} %cotangent.1, f32[2,768]{1,0:T(2,128)} %gains.5, ...), custom_call_target="tpu_custom_call" | custom-call | tf_op jit(solution)/shard_map/feed/pallas_call | solution.py:419
  219.0 10.4 %attend_back.1 = (bf16[1152,768]{1,0:T(8,128)(2,1)}, bf16[1152,768]{1,0:T(8,128)(2,1)}, bf16[1152,768]{1,0:T(8,128)(2,1)}) custom-call(s32[7]{0:T(128)} %groups.9, bf16[1152,2304]{1,0:T(8,128)(2,1)} %get-tuple-element.19.q_ref.k_ref.v_ref, bf16[1152,2304]{1,0:T(8,128)(2,1)} %get-tuple-element.19.q_ref.k_ref.v_ref, ...), custom_call_target="tpu_custom_call" | custom-call | tf_op jit(solution)/shard_map/attend_back/pallas_call | solution.py:347
  229.4 1.5 copy-done.4
  230.9 1.5 copy-done.5
  232.4 11.9 %finish.1 = (bf16[1152,768]{1,0:T(8,128)(2,1)}, f32[64,768]{1,0:T(8,128)S(1)}) custom-call(s32[7]{0:T(128)S(1)} %copy-done.13, f32[1152,768]{1,0:T(8,128)} %copy-done.1, f32[1152,768]{1,0:T(8,128)} %get-tuple-element.22.middle_grad, bf16[1152,768]{1,0:T(8,128)(2,1)S(1)} %copy-done.4, bf16[1152,768]{1,0:T(8,128)(2,1)S(1)} %copy-done.5, ...), custom_call_target="tpu_custom_call" | custom-call | tf_op jit(solution)/shard_map/finish/pallas_call | solution.py:480
  244.2 0.7 copy-done.9
  244.9 31.5 %share.1 = (f32[50,768]{1,0:T(8,128)}, f32[1,1]{1,0:T(1,128)}) custom-call(f32[64,768]{1,0:T(8,128)} %copy-done.9, f32[50,768]{1,0:T(8,128)} %prompts.3), custom_call_target="tpu_custom_call" | custom-call | tf_op jit(solution)/shard_map/share/pallas_call | solution.py:599
  276.4 1.6 copy.18
  (26 shorter events, 0.2 us)
Async XLA Ops:
  7.2 2.9 %copy-start.14 = (s32[1152,2]{0,1:T(2,128)S(1)}, s32[1152,2]{0,1:T(2,128)}, u32[]{:S(2)}) copy-start(s32[1152,2]{0,1:T(2,128)} %param.12) | copy-start | bytes 27652
  7.2 46.8 %copy-start.12 = (s32[7]{0:T(128)S(1)}, s32[7]{0:T(128)}, u32[]{:S(2)}) copy-start(s32[7]{0:T(128)} %groups.9) | copy-start | bytes 88
  7.2 46.8 %copy-start.10 = (f32[2,768]{1,0:T(2,128)S(1)}, f32[2,768]{1,0:T(2,128)}, u32[]{:S(2)}) copy-start(f32[2,768]{1,0:T(2,128)} %gains.5) | copy-start | bytes 18436
  7.2 46.8 %copy-start.6 = (f32[50,768]{1,0:T(8,128)S(1)}, f32[50,768]{1,0:T(8,128)}, u32[]{:S(2)}) copy-start(f32[50,768]{1,0:T(8,128)} %prompts.3) | copy-start | bytes 460804
  7.2 46.8 %copy-start.7 = (bf16[197,768]{1,0:T(8,128)(2,1)S(1)}, bf16[197,768]{1,0:T(8,128)(2,1)}, u32[]{:S(2)}) copy-start(bf16[197,768]{1,0:T(8,128)(2,1)} %pos_table.1) | copy-start | bytes 907780
  7.2 46.8 %copy-start.3 = (bf16[1152,768]{1,0:T(8,128)(2,1)S(1)}, bf16[1152,768]{1,0:T(8,128)(2,1)}, u32[]{:S(2)}) copy-start(bf16[1152,768]{1,0:T(8,128)(2,1)} %tokens.1) | copy-start | bytes 5308420
  7.2 46.7 %all-gather.5.cloned.1.call-start = ((), (), s32[]{:S(2)}) async-start(), calls=%async_computation | async-start | bytes 3981312 | tf_op jit(solution)/shard_map/all_gather | solution.py:636
  8.0 69.2 %all-gather.7.cloned.1.call-start = ((), (), s32[]{:S(2)}) async-start(), calls=%async_computation.1 | async-start | bytes 1327104 | tf_op jit(solution)/shard_map/all_gather | solution.py:637
  8.7 121.6 %all-gather.9.cloned.1.call-start = ((), (), s32[]{:S(2)}) async-start(), calls=%async_computation.2 | async-start | bytes 5308416 | tf_op jit(solution)/shard_map/all_gather | solution.py:638
  9.4 172.9 %all-gather.11.cloned.1.call-start = ((), (), s32[]{:S(2)}) async-start(), calls=%async_computation.3 | async-start | bytes 5308416 | tf_op jit(solution)/shard_map/all_gather | solution.py:639
  54.0 2.0 copy-start
  65.6 1.8 copy-start.1
  73.7 1.2 copy-start.2
  74.9 0.7 copy-start.8
  218.9 10.4 %copy-start.11 = (f32[2,768]{1,0:T(2,128)S(1)}, f32[2,768]{1,0:T(2,128)}, u32[]{:S(2)}) copy-start(f32[2,768]{1,0:T(2,128)} %gains.5) | copy-start | bytes 18436
  218.9 10.4 %copy-start.13 = (s32[7]{0:T(128)S(1)}, s32[7]{0:T(128)}, u32[]{:S(2)}) copy-start(s32[7]{0:T(128)} %groups.9) | copy-start | bytes 88
  229.4 1.5 copy-start.4
  230.9 1.5 copy-start.5
  244.2 0.7 copy-start.9
Sparse Core Ops, SparseCore 0:
  9.7 44.2 all-gather.4
  55.6 21.5 all-gather.6
  78.8 51.4 all-gather.8
  131.8 50.5 all-gather.10

commit v3 on v2

--- a/solution.py
+++ b/solution.py
@@ -81,24 +81,19 @@
     ) * rstd
 
 
-def embed_kernel(
-    slots, groups, tokens, pos_index, pos_table, prompts, gains, w_qkv, hidden_out, qkv_out, table
-):
-    tile = tokens.shape[0]
-    step = pl.program_id(0)
-
-    @pl.when(step == 0)
-    def _():
-        table[...] = jnp.zeros_like(table)
-        table[: pos_table.shape[0]] = pos_table[...]
-        rest = prompts[...]
-        for piece in range(3):
-            part = rest.astype(BF)
-            first = POS_ROWS + piece * SLOT_ROWS
-            table[first : first + PROMPTS] = part
-            rest = rest - part.astype(F32)
-
-    prompt_slot, _ = row_places(groups, slots, step * tile, tile)
+def fill_table(table, pos_table, prompts):
+    table[...] = jnp.zeros_like(table)
+    table[: pos_table.shape[0]] = pos_table[...]
+    rest = prompts[...]
+    for piece in range(3):
+        part = rest.astype(BF)
+        first = POS_ROWS + piece * SLOT_ROWS
+        table[first : first + PROMPTS] = part
+        rest = rest - part.astype(F32)
+
+
+def embedded(groups, slots, first_row, tokens, pos_index, table):
+    prompt_slot, _ = row_places(groups, slots, first_row, tokens.shape[0])
     is_prompt = prompt_slot >= 0
     lane = lax.broadcasted_iota(jnp.int32, (1, POS_ROWS), 1)
     left = jnp.where(is_prompt, -1, pos_index[:, 0:1])
@@ -110,7 +105,20 @@
     picked = dot(half_hot.astype(BF), table[:POS_ROWS]) + dot(
         slot_hot.astype(BF), table[POS_ROWS:]
     )
-    hidden = jnp.where(is_prompt, 0.0, tokens[...].astype(F32)) + picked
+    return jnp.where(is_prompt, 0.0, tokens.astype(F32)) + picked
+
+
+def embed_kernel(
+    slots, groups, tokens, pos_index, pos_table, prompts, gains, w_qkv, hidden_out, qkv_out, table
+):
+    tile = tokens.shape[0]
+    step = pl.program_id(0)
+
+    @pl.when(step == 0)
+    def _():
+        fill_table(table, pos_table, prompts)
+
+    hidden = embedded(groups, slots, step * tile, tokens[...], pos_index[...], table)
     hidden_out[...] = hidden
     normal, _ = norm_parts(hidden)
     normed = (normal * gains[0:1]).astype(BF)
@@ -146,6 +154,390 @@
         compiler_params=pltpu.CompilerParams(vmem_limit_bytes=40 << 20),
         name="embed",
     )(size_group, tokens, pos_index, pos_table, prompts, gains, w_qkv)
+
+
+class Gather:
+    def __init__(self, place, index, full, sems, by_rows=False):
+        self.dp, self.wide, self.planes, self.plane, self.core = place
+        self.index = index
+        self.full = full
+        self.send, self.recv = sems
+        self.rows = full.shape[0] // (2 * self.planes)
+        self.columns = full.shape[1] // 8
+        self.by_rows = by_rows
+        d = self.dp
+        self.across = d + 1 - 2 * lax.rem(d, 2)
+        self.beyond = lax.rem(d + 2, 4)
+
+    def alpha(self, d):
+        return d
+
+    def beta(self, d):
+        return 4 + 2 * lax.rem(d, 2) + d // 2
+
+    def pair(self, slot):
+        return slot - lax.rem(slot, 2)
+
+    def shard(self, plane, core, slot=None, count=1, array=None):
+        full = self.full if array is None else array
+        first = pl.multiple_of((2 * plane + core) * self.rows, self.rows)
+        if slot is None:
+            return full.at[pl.ds(first, self.rows)]
+        if self.by_rows:
+            step = self.rows // 8
+            return full.at[pl.ds(pl.multiple_of(first + slot * step, step), count * step)]
+        column = pl.multiple_of(slot * self.columns, self.columns)
+        return full.at[pl.ds(first, self.rows), pl.ds(column, count * self.columns)]
+
+    def copy(self, ref, send, recv, device):
+        return pltpu.make_async_remote_copy(
+            ref,
+            ref,
+            self.send.at[self.index, send],
+            self.recv.at[self.index, recv],
+            device_id=device,
+            device_id_type=MESH,
+        )
+
+    def device(self, plane):
+        return (self.dp, 2 * plane + self.core)
+
+    def nearest(self, k):
+        n = self.planes
+        low = 1 - self.plane // (n // 2)
+        edge = low * self.plane + (1 - low) * (n - 1 - self.plane)
+        other = k + 1 - (edge - k + n - 1) // n
+        return low * other + (1 - low) * (n - 1 - other)
+
+    def along_copies(self, plane):
+        n = self.planes
+        up = (plane <= self.plane) & (self.plane < n - 1)
+        down = (plane >= self.plane) & (self.plane > 0)
+        for part, slot in enumerate((self.alpha(self.dp), self.beta(self.dp))):
+            ref = self.shard(plane, self.core, slot)
+            sem = 2 * plane + part
+            for go, sent, target in (
+                (up, sem, lax.rem(self.plane + 1, n)),
+                (down, 2 * n + sem, lax.rem(self.plane + n - 1, n)),
+            ):
+                yield go, self.copy(ref, sent, sem, self.device(target))
+
+    def along(self, plane):
+        for go, copy in self.along_copies(plane):
+            pl.when(go)(copy.start)
+
+    def wait_along(self, plane):
+        for part, slot in enumerate((self.alpha(self.dp), self.beta(self.dp))):
+            ref = self.shard(plane, self.core, slot)
+            sem = 2 * plane + part
+            self.copy(ref, sem, sem, self.device(plane)).wait_recv()
+
+    def exchange_copies(self, plane):
+        for part, (slot, d) in enumerate(
+            ((self.alpha(self.dp), self.across), (self.beta(self.dp), self.beyond))
+        ):
+            sem = 4 * self.planes + 2 * plane + part
+            yield self.copy(self.shard(plane, self.core, slot), sem, sem, (d, self.wide))
+
+    def exchange(self, plane):
+        for copy in self.exchange_copies(plane):
+            copy.start()
+
+    def wait_exchange(self, plane):
+        for part, (slot, d) in enumerate(
+            ((self.alpha(self.across), self.across), (self.beta(self.beyond), self.beyond))
+        ):
+            sem = 4 * self.planes + 2 * plane + part
+            self.copy(self.shard(plane, self.core, slot), sem, sem, (d, self.wide)).wait_recv()
+
+    def pair_copies(self, plane):
+        for part, (slot, d) in enumerate(
+            ((self.alpha(self.dp), self.beyond), (self.beta(self.dp), self.across))
+        ):
+            sem = 6 * self.planes + 2 * plane + part
+            ref = self.shard(plane, self.core, self.pair(slot), 2)
+            yield self.copy(ref, sem, sem, (d, self.wide))
+
+    def exchange_pairs(self, plane):
+        for copy in self.pair_copies(plane):
+            copy.start()
+
+    def wait_pairs(self, plane):
+        for part, (slot, d) in enumerate(
+            ((self.alpha(self.beyond), self.beyond), (self.beta(self.across), self.across))
+        ):
+            sem = 6 * self.planes + 2 * plane + part
+            ref = self.shard(plane, self.core, self.pair(slot), 2)
+            self.copy(ref, sem, sem, (d, self.wide)).wait_recv()
+
+    def other_core(self):
+        return (self.dp, 2 * self.plane + 1 - self.core)
+
+    def give_copy(self, plane):
+        sem = 8 * self.planes + plane
+        return self.copy(self.shard(plane, self.core), sem, sem, self.other_core())
+
+    def give(self, plane):
+        self.give_copy(plane).start()
+
+    def wait_all_given(self):
+        for plane in range(self.planes):
+            sem = 8 * self.planes + plane
+            self.copy(self.shard(plane, 1 - self.core), sem, sem, self.other_core()).wait_recv()
+
+    def begin(self):
+        self.along(self.plane)
+        self.give(self.plane)
+
+    def fetch(self, k):
+        plane = self.nearest(k)
+        self.wait_along(plane)
+        self.along(plane)
+
+    def bring(self, k):
+        self.fetch(k)
+        self.exchange(self.nearest(k))
+
+    def pass_on(self, k):
+        plane = self.nearest(k)
+        self.wait_exchange(plane)
+        self.exchange_pairs(plane)
+
+    def close(self, k):
+        plane = self.nearest(k)
+        self.wait_pairs(plane)
+        self.give(plane)
+
+    def wait_fetched(self):
+        for k in range(self.planes):
+            plane = self.plane if k == self.planes - 1 else self.nearest(k)
+            for go, copy in self.along_copies(plane):
+                pl.when(go)(copy.wait_send)
+
+    def wait_passed(self):
+        self.give_copy(self.plane).wait_send()
+        for k in range(self.planes - 1):
+            plane = self.nearest(k)
+            for copy in self.exchange_copies(plane):
+                copy.wait_send()
+            for copy in self.pair_copies(plane):
+                copy.wait_send()
+            self.give_copy(plane).wait_send()
+
+    def greet(self, planes=True):
+        barrier = pltpu.get_barrier_semaphore()
+        peers = [(self.across, self.wide), (self.beyond, self.wide), self.other_core()]
+        if planes:
+            peers += [
+                self.device(lax.rem(self.plane + step, self.planes))
+                for step in range(1, self.planes)
+            ]
+        for device in peers:
+            pl.semaphore_signal(barrier, inc=1, device_id=device, device_id_type=MESH)
+        return barrier, len(peers)
+
+    def fetched(self, k, array=None):
+        plane = self.nearest(k)
+        slots = (self.alpha(self.dp), self.beta(self.dp))
+        return [self.shard(plane, self.core, slot, 1, array) for slot in slots]
+
+    @staticmethod
+    def semaphores(planes):
+        return 9 * planes
+
+
+def gather_embed_kernel(
+    planes,
+    slots,
+    groups,
+    pos_table,
+    prompts,
+    gains,
+    tokens_in,
+    pos_index_in,
+    own_qkv,
+    own_out,
+    own_up,
+    own_down,
+    hidden_out,
+    qkv_out,
+    full_qkv,
+    full_out,
+    full_up,
+    part_down,
+    table,
+    tokens,
+    pos_index,
+    hidden,
+    normed,
+    qkv,
+    first_full,
+    second_full,
+    third_full,
+    send,
+    recv,
+    local,
+):
+    d = lax.axis_index("dp")
+    w = lax.axis_index("wide")
+    place = (d, w, planes, w // 2, lax.rem(w, 2))
+    first = Gather(place, 0, first_full, (send, recv))
+    second = Gather(place, 1, second_full, (send, recv))
+    third = Gather(place, 2, third_full, (send, recv), by_rows=True)
+    others = planes - 1
+    qkv_columns = own_qkv.shape[1]
+    barrier, greeted = first.greet()
+    mine = pl.ds(pl.multiple_of(w * first.rows, first.rows), first.rows)
+    loads = [
+        pltpu.make_async_copy(own_qkv, first_full.at[mine, :qkv_columns], local.at[0]),
+        pltpu.make_async_copy(own_out, first_full.at[mine, qkv_columns:], local.at[1]),
+        pltpu.make_async_copy(own_up, second_full.at[mine], local.at[2]),
+        pltpu.make_async_copy(own_down, third.shard(third.plane, third.core), local.at[3]),
+        pltpu.make_async_copy(tokens_in, tokens, local.at[4]),
+        pltpu.make_async_copy(pos_index_in, pos_index, local.at[5]),
+    ]
+    for copy in loads:
+        copy.start()
+    fill_table(table, pos_table, prompts)
+    for copy in loads[:4]:
+        copy.wait()
+    pl.semaphore_wait(barrier, greeted)
+    first.begin()
+    second.begin()
+    for copy in loads[4:]:
+        copy.wait()
+
+    rows = tokens.shape[0]
+    tiles = 6
+    tile = rows // tiles
+    outgoing = []
+
+    def leave(source, target):
+        copy = pltpu.make_async_copy(source, target, local.at[6 + len(outgoing)])
+        copy.start()
+        outgoing.append(copy)
+
+    def embed_tile(index):
+        part = slice(index * tile, (index + 1) * tile)
+        value = embedded(groups, slots, index * tile, tokens[part], pos_index[part], table)
+        hidden[part] = value
+        leave(hidden.at[part], hidden_out.at[part])
+        normal, _ = norm_parts(value)
+        normed[part] = (normal * gains[0:1]).astype(BF)
+
+    def qkv_tile(index):
+        part = slice(index * tile, (index + 1) * tile)
+        qkv[part] = dot(normed[part], first_full[:, :qkv_columns]).astype(BF)
+        leave(qkv.at[part], qkv_out.at[part])
+
+    embed_tile(0)
+    embed_tile(1)
+    first.bring(0)
+    embed_tile(2)
+    first.bring(1)
+    first.pass_on(0)
+    embed_tile(3)
+    first.bring(2)
+    first.pass_on(1)
+    embed_tile(4)
+    third.along(third.plane)
+    second.bring(0)
+    first.pass_on(2)
+    first.close(0)
+    embed_tile(5)
+    second.bring(1)
+    second.pass_on(0)
+    first.close(1)
+    second.bring(2)
+    second.pass_on(1)
+    first.close(2)
+    first.wait_all_given()
+    leave(first_full.at[:, :qkv_columns], full_qkv)
+    leave(first_full.at[:, qkv_columns:], full_out)
+    qkv_tile(0)
+    second.pass_on(2)
+    second.close(0)
+    qkv_tile(1)
+    third.fetch(0)
+    qkv_tile(2)
+    second.close(1)
+    third.fetch(1)
+    qkv_tile(3)
+    third.fetch(2)
+    qkv_tile(4)
+    for k in range(others):
+        for source, target in zip(third.fetched(k), third.fetched(k, part_down)):
+            leave(source, target)
+    qkv_tile(5)
+    second.close(2)
+    second.wait_all_given()
+    leave(second_full, full_up)
+    first.wait_fetched()
+    second.wait_fetched()
+    third.wait_fetched()
+    first.wait_passed()
+    second.wait_passed()
+    for copy in outgoing:
+        copy.wait()
+
+
+def can_gather(axes, w_qkv, w_out, w_up, w_down):
+    return (
+        axes["dp"] == 4
+        and axes["wide"] % 4 == 0
+        and w_qkv.shape[0] % 16 == 0
+        and w_down.shape[0] % (8 * 16) == 0
+        and w_up.shape[1] % (8 * LANES) == 0
+        and (w_qkv.shape[1] + w_out.shape[1]) % (8 * LANES) == 0
+    )
+
+
+def gather_embed(
+    axes, size_group, tokens, pos_index, pos_table, prompts, gains, w_qkv, w_out, w_up, w_down
+):
+    rows, width = tokens.shape
+    wide = axes["wide"]
+    planes = wide // 2
+    depth = w_qkv.shape[0] * wide
+    inner_width = w_up.shape[1]
+    vmem = pl.BlockSpec(memory_space=pltpu.VMEM)
+    hbm = pl.BlockSpec(memory_space=pltpu.HBM)
+    dma = pltpu.SemaphoreType.DMA
+    count = Gather.semaphores(planes)
+    first_columns = w_qkv.shape[1] + w_out.shape[1]
+    return pl.pallas_call(
+        functools.partial(gather_embed_kernel, planes, size_group.shape[0]),
+        in_specs=[pl.BlockSpec(memory_space=pltpu.SMEM)] + [vmem] * 3 + [hbm] * 6,
+        out_specs=[hbm] * 6,
+        out_shape=[
+            jax.ShapeDtypeStruct((rows, width), F32),
+            jax.ShapeDtypeStruct((rows, w_qkv.shape[1]), BF),
+            jax.ShapeDtypeStruct((depth, w_qkv.shape[1]), BF),
+            jax.ShapeDtypeStruct((depth, w_out.shape[1]), BF),
+            jax.ShapeDtypeStruct((depth, inner_width), BF),
+            jax.ShapeDtypeStruct((inner_width, width), BF),
+        ],
+        scratch_shapes=[
+            pltpu.VMEM((POS_ROWS + 3 * SLOT_ROWS, width), BF),
+            pltpu.VMEM((rows, width), BF),
+            pltpu.VMEM((rows, 2), jnp.int32),
+            pltpu.VMEM((rows, width), F32),
+            pltpu.VMEM((rows, width), BF),
+            pltpu.VMEM((rows, w_qkv.shape[1]), BF),
+            pltpu.VMEM((depth, first_columns), BF),
+            pltpu.VMEM((depth, inner_width), BF),
+            pltpu.VMEM((inner_width, width), BF),
+            dma((3, count)),
+            dma((3, count)),
+            dma((6 + 12 + 3 + 2 * (planes - 1),)),
+        ],
+        compiler_params=pltpu.CompilerParams(
+            collective_id=0, has_side_effects=True, vmem_limit_bytes=56 << 20
+        ),
+        name="gather_embed",
+    )(
+        size_group, pos_table, prompts, gains, tokens, pos_index, w_qkv, w_out, w_up, w_down
+    )
 
 
 def half(values, which):
@@ -432,6 +824,200 @@
         compiler_params=pltpu.CompilerParams(vmem_limit_bytes=56 << 20),
         name="feed",
     )(size_group, hidden, mixed, cotangent, gains, w_out, w_up, w_down)
+
+
+def gather_feed_kernel(
+    planes,
+    slots,
+    chunk,
+    groups,
+    gains,
+    hidden_in,
+    mixed_in,
+    cotangent_in,
+    full_out,
+    full_up,
+    own_down,
+    part_down,
+    out_ref,
+    middle_grad_ref,
+    mixed_grad_ref,
+    middle,
+    mixed,
+    cotangent,
+    w_out,
+    w_up,
+    w_down,
+    active,
+    slope,
+    send,
+    recv,
+    weights_in,
+    rows_in,
+    rows_out,
+):
+    d = lax.axis_index("dp")
+    w = lax.axis_index("wide")
+    down = Gather((d, w, planes, w // 2, lax.rem(w, 2)), 0, w_down, (send, recv), by_rows=True)
+    barrier, greeted = down.greet(planes=False)
+    others = planes - 1
+    tiles = rows_in.shape[0]
+    tile = middle.shape[0] // tiles
+    inner_width = w_up.shape[1]
+
+    def tile_rows(index):
+        return pl.ds(pl.multiple_of(index * tile, tile), tile)
+
+    def loads(index):
+        part = tile_rows(index)
+        return [
+            pltpu.make_async_copy(hidden_in.at[part], middle.at[part], rows_in.at[index, 0]),
+            pltpu.make_async_copy(mixed_in.at[part], mixed.at[part], rows_in.at[index, 1]),
+            pltpu.make_async_copy(cotangent_in.at[part], cotangent.at[part], rows_in.at[index, 2]),
+        ]
+
+    def stores(index):
+        part = tile_rows(index)
+        return [
+            pltpu.make_async_copy(middle.at[part], middle_grad_ref.at[part], rows_out.at[index, 0]),
+            pltpu.make_async_copy(mixed.at[part], mixed_grad_ref.at[part], rows_out.at[index, 1]),
+            pltpu.make_async_copy(cotangent.at[part], out_ref.at[part], rows_out.at[index, 2]),
+        ]
+
+    down_loads = [(own_down, down.shard(down.plane, down.core))]
+    for k in range(others):
+        down_loads += list(zip(down.fetched(k, part_down), down.fetched(k)))
+    down_loads = [
+        pltpu.make_async_copy(source, target, weights_in.at[2 + index])
+        for index, (source, target) in enumerate(down_loads)
+    ]
+    out_load = pltpu.make_async_copy(full_out, w_out, weights_in.at[0])
+    up_load = pltpu.make_async_copy(full_up, w_up, weights_in.at[1])
+    for copy in down_loads:
+        copy.start()
+    out_load.start()
+    for copy in loads(0):
+        copy.start()
+    up_load.start()
+    for index in range(1, tiles):
+        for copy in loads(index):
+            copy.start()
+    for copy in down_loads:
+        copy.wait()
+    pl.semaphore_wait(barrier, greeted)
+    for k in range(others):
+        down.exchange(down.nearest(k))
+    down.give(down.plane)
+    out_load.wait()
+    up_load.wait()
+    gain = gains[1:2]
+
+    def pump(step):
+        @pl.when((step >= 0) & (step < others))
+        def _():
+            down.pass_on(step)
+
+        @pl.when((step >= 2) & (step < others + 2))
+        def _():
+            down.close(step - 2)
+
+    def up_tile(index, carry):
+        for copy in loads(index):
+            copy.wait()
+        part = tile_rows(index)
+        value = middle[part, :] + dot(mixed[part, :], w_out[...])
+        middle[part, :] = value
+        normal, _ = norm_parts(value)
+        second = (normal * gain).astype(BF)
+        for first in range(0, inner_width, chunk):
+            columns = slice(first, first + chunk)
+            inner = dot(second, w_up[:, columns])
+            phi = 0.5 + 0.5 * lax.erf(inner * (0.5**0.5))
+            density = jnp.exp2(inner * inner * (-0.5 * LOG2E)) * 0.3989422804014327
+            active[part, columns] = (inner * phi).astype(BF)
+            slope[part, columns] = phi + inner * density
+            if first + chunk == inner_width // 2:
+                pump(2 * index)
+        pump(2 * index + 1)
+        return carry
+
+    lax.fori_loop(0, tiles, up_tile, 0)
+    for step in range(2 * tiles, others + 2):
+        pump(step)
+    down.wait_all_given()
+    total = total_length(groups, slots)
+
+    def down_tile(index, carry):
+        part = tile_rows(index)
+        rows = index * tile + lax.broadcasted_iota(jnp.int32, (tile, 1), 0)
+        live = rows < total
+        out_grad = jnp.where(live, cotangent[part, :].astype(F32), 0.0)
+        out_grad_low = out_grad.astype(BF)
+        value = middle[part, :]
+        back = jnp.zeros_like(value)
+        for first in range(0, inner_width, chunk):
+            columns = slice(first, first + chunk)
+            act_grad = dot(out_grad_low, w_down[columns], NT)
+            inner_grad = (act_grad * slope[part, columns]).astype(BF)
+            back = back + dot(inner_grad, w_up[:, columns], NT)
+        forward = value + dot(active[part, :], w_down[...])
+        cotangent[part, :] = jnp.where(live, forward, 0.0).astype(BF)
+        normal, rstd = norm_parts(value)
+        middle_grad = out_grad + norm_back(normal, rstd, gain, back)
+        middle[part, :] = middle_grad
+        mixed[part, :] = dot(middle_grad.astype(BF), w_out[...], NT).astype(BF)
+        for copy in stores(index):
+            copy.start()
+        return carry
+
+    lax.fori_loop(0, tiles, down_tile, 0)
+    down.wait_passed()
+    for index in range(tiles):
+        for copy in stores(index):
+            copy.wait()
+
+
+def gather_feed(axes, size_group, hidden, mixed, cotangent, gains, w_out, w_up, w_down, part_down):
+    rows, width = hidden.shape
+    planes = axes["wide"] // 2
+    inner_width = w_up.shape[1]
+    tiles = 3
+    hbm = pl.BlockSpec(memory_space=pltpu.HBM)
+    dma = pltpu.SemaphoreType.DMA
+    count = Gather.semaphores(planes)
+    return pl.pallas_call(
+        functools.partial(gather_feed_kernel, planes, size_group.shape[0], 512),
+        in_specs=[
+            pl.BlockSpec(memory_space=pltpu.SMEM),
+            pl.BlockSpec(memory_space=pltpu.VMEM),
+        ]
+        + [hbm] * 7,
+        out_specs=[hbm] * 3,
+        out_shape=[
+            jax.ShapeDtypeStruct((rows, width), BF),
+            jax.ShapeDtypeStruct((rows, width), F32),
+            jax.ShapeDtypeStruct((rows, width), BF),
+        ],
+        scratch_shapes=[
+            pltpu.VMEM((rows, width), F32),
+            pltpu.VMEM((rows, width), BF),
+            pltpu.VMEM((rows, width), BF),
+            pltpu.VMEM(w_out.shape, BF),
+            pltpu.VMEM(w_up.shape, BF),
+            pltpu.VMEM((inner_width, width), BF),
+            pltpu.VMEM((rows, inner_width), BF),
+            pltpu.VMEM((rows, inner_width), F32),
+            dma((1, count)),
+            dma((1, count)),
+            dma((3 + 2 * (planes - 1),)),
+            dma((tiles, 3)),
+            dma((tiles, 3)),
+        ],
+        compiler_params=pltpu.CompilerParams(
+            collective_id=2, has_side_effects=True, vmem_limit_bytes=58 << 20
+        ),
+        name="gather_feed",
+    )(size_group, gains, hidden, mixed, cotangent, w_out, w_up, w_down, part_down)
 
 
 def finish_kernel(
@@ -633,15 +1219,43 @@
     w_down,
     cotangent,
 ):
-    full_qkv = lax.all_gather(w_qkv, "wide", axis=0, tiled=True)
-    full_out = lax.all_gather(w_out, "wide", axis=0, tiled=True)
-    full_up = lax.all_gather(w_up, "wide", axis=0, tiled=True)
-    full_down = lax.all_gather(w_down, "wide", axis=0, tiled=True)
-    hidden, qkv = embed(size_group, tokens, pos_index, pos_table, prompts, norm_gains, full_qkv)
-    mixed, totals = attend(size_group, qkv)
-    outputs, middle_grad, mixed_grad = feed(
-        size_group, hidden, mixed, cotangent, norm_gains, full_out, full_up, full_down
-    )
+    if can_gather(axes, w_qkv, w_out, w_up, w_down):
+        hidden, qkv, full_qkv, full_out, full_up, part_down = gather_embed(
+            axes,
+            size_group,
+            tokens,
+            pos_index,
+            pos_table,
+            prompts,
+            norm_gains,
+            w_qkv,
+            w_out,
+            w_up,
+            w_down,
+        )
+        mixed, totals = attend(size_group, qkv)
+        outputs, middle_grad, mixed_grad = gather_feed(
+            axes,
+            size_group,
+            hidden,
+            mixed,
+            cotangent,
+            norm_gains,
+            full_out,
+            full_up,
+            w_down,
+            part_down,
+        )
+    else:
+        full_qkv = lax.all_gather(w_qkv, "wide", axis=0, tiled=True)
+        full_out = lax.all_gather(w_out, "wide", axis=0, tiled=True)
+        full_up = lax.all_gather(w_up, "wide", axis=0, tiled=True)
+        full_down = lax.all_gather(w_down, "wide", axis=0, tiled=True)
+        hidden, qkv = embed(size_group, tokens, pos_index, pos_table, prompts, norm_gains, full_qkv)
+        mixed, totals = attend(size_group, qkv)
+        outputs, middle_grad, mixed_grad = feed(
+            size_group, hidden, mixed, cotangent, norm_gains, full_out, full_up, full_down
+        )
     dq, dk, dv = attend_back(size_group, qkv, mixed_grad, mixed, totals)
     input_grad, sums = finish(size_group, hidden, middle_grad, dq, dk, dv, norm_gains, full_qkv)
     prompt_grad, penalty = share(axes, sums, prompts)

time: 287 us -> 180 us (0.63)
  waiting for transfers between devices: 153 us -> 0 us
  Pallas kernels: 106 us -> 169 us
  between operations: 15.6 us -> 2.44 us
    all_gather x4 -> x0, waiting for transfers between devices: 150 us -> none  [the longest x1 53.1 us: shards(): full_up = lax.all_gather(w_up, 'wide', axis=0, tiled=True)]
    pallas_call x2, Pallas kernels: 46.2 us -> 109 us  [the longest x1 55.8 us: gather_feed(): pl.pallas_call(functools.partial(gather_feed_kernel, planes, size_group.s...]
    unnamed x32 -> x23, local copies, waits for them, and re-layouts: 11.2 us -> 9.18 us
  transfers between devices with their start and end apart: 4 -> 0, of which waited for: 4 -> 0; matrix products, arithmetic and copies ran while one was open for 0% -> 0% of each run, Pallas kernels for 6% -> 0%
where the time goes in v3:
time: 180 us; the launch traced here: 181 us
  Pallas kernels  169 us (94%)
  local copies, waits for them, and re-layouts  9.18 us (5%)
  between operations  2.44 us (1%)
    pallas_call x1, Pallas kernels, gather_feed(): pl.pallas_call(functools.partial(gather_feed_kernel, planes, size_group.s...  55.8 us
    pallas_call x1, Pallas kernels, gather_embed(): pl.pallas_call(functools.partial(gather_embed_kernel, planes, size_group....  53.3 us
    pallas_call x1, Pallas kernels, share(): pl.pallas_call(functools.partial(share_kernel, dp, wide), in_specs=[pl.Bl...  31.4 us
    pallas_call x1, Pallas kernels, finish(): pl.pallas_call(functools.partial(finish_kernel, size_group.shape[0]), gri...  11.9 us
    pallas_call x1, Pallas kernels, attend_back(): pl.pallas_call(functools.partial(attend_back_kernel, slots), grid_spec=pl...  10.3 us
    unnamed x23, local copies, waits for them, and re-layouts  9.18 us
    pallas_call x1, Pallas kernels, attend(): pl.pallas_call(functools.partial(attend_kernel, slots), grid_spec=pltpu.P...  6.34 us

profile of v3, /device:TPU:0, one launch (start us, length us, event | category | flops | bytes accessed | tf_op | source)
XLA Modules:
  0.0 180.7 jit_solution(3757596257522648893)
XLA Ops:
  0.6 1.8 copy.15.pos_index_in
  2.4 53.3 %gather_embed.1 = (f32[1152,768]{1,0:T(8,128)}, bf16[1152,2304]{1,0:T(8,128)(2,1)}, bf16[768,2304]{1,0:T(8,128)(2,1)}, bf16[768,768]{1,0:T(8,128)(2,1)}, bf16[76...) custom-call(s32[7]{0:T(128)} %groups.9, bf16[197,768]{1,0:T(8,128)(2,1)} %pos_table.1, f32[50,768]{1,0:T(8,128)} %prompts.3, ...), custom_call_target="tpu_custom_call" | custom-call | tf_op jit(solution)/shard_map/gather_embed/pallas_call | solution.py:508
  55.7 0.0 copy-done.6
  55.7 6.3 %attend.1 = (bf16[1152,768]{1,0:T(8,128)(2,1)S(1)}, f32[3,28,1,640]{3,2,1,0:T(1,128)S(1)}) custom-call(s32[7]{0:T(128)S(1)} %copy-done.6, bf16[1152,2304]{1,0:T(8,128)(2,1)} %get-tuple-element.23.q_ref.k_ref.v_ref, bf16[1152,2304]{1,0:T(8,128)(2,1)} %get-tuple-element.23.q_ref.k_ref.v_ref, bf16[1152,2304]{1,0:T(8,128)(2,1)} %get-tuple-element.23.q_ref.k_ref.v_ref), custom_call_target="tpu_custom_call" | custom-call | tf_op jit(solution)/shard_map/attend/pallas_call | solution.py:637
  62.1 0.0 copy-start
  62.1 1.2 copy-done
  63.3 0.7 copy-done.3
  64.0 55.8 %gather_feed.1 = (bf16[1152,768]{1,0:T(8,128)(2,1)}, f32[1152,768]{1,0:T(8,128)}, bf16[1152,768]{1,0:T(8,128)(2,1)}) custom-call(s32[7]{0:T(128)} %groups.9, f32[2,768]{1,0:T(2,128)} %gains.5, f32[1152,768]{1,0:T(8,128)} %get-tuple-element.22.hidden_in.hidden, bf16[1152,768]{1,0:T(8,128)(2,1)} %copy-done, bf16[1152,768]{1,0:T(8,128)(2,1)} %cotangent_in.1, ...), custom_call_target="tpu_custom_call" | custom-call | tf_op jit(solution)/shard_map/gather_feed/pallas_call | solution.py:988
  119.8 0.0 copy-start.5
  119.8 0.0 copy-start.7
  119.8 10.3 %attend_back.1 = (bf16[1152,768]{1,0:T(8,128)(2,1)}, bf16[1152,768]{1,0:T(8,128)(2,1)}, bf16[1152,768]{1,0:T(8,128)(2,1)}) custom-call(s32[7]{0:T(128)} %groups.9, bf16[1152,2304]{1,0:T(8,128)(2,1)} %get-tuple-element.23.q_ref.k_ref.v_ref, bf16[1152,2304]{1,0:T(8,128)(2,1)} %get-tuple-element.23.q_ref.k_ref.v_ref, ...), custom_call_target="tpu_custom_call" | custom-call | tf_op jit(solution)/shard_map/attend_back/pallas_call | solution.py:739
  130.1 0.0 copy-done.5
  130.1 0.0 copy-done.7
  130.1 0.0 copy-start.1
  130.1 1.5 copy-done.1
  131.6 1.5 copy-done.2
  133.1 11.9 %finish.1 = (bf16[1152,768]{1,0:T(8,128)(2,1)}, f32[64,768]{1,0:T(8,128)S(1)}) custom-call(s32[7]{0:T(128)S(1)} %copy-done.7, f32[1152,768]{1,0:T(8,128)} %get-tuple-element.22.hidden_in.hidden, f32[1152,768]{1,0:T(8,128)} %get-tuple-element.29.middle_grad, bf16[1152,768]{1,0:T(8,128)(2,1)S(1)} %copy-done.1, bf16[1152,768]{1,0:T(8,128)(2,1)S(1)} %copy-done.2, ...), custom_call_target="tpu_custom_call" | custom-call | tf_op jit(solution)/shard_map/finish/pallas_call | solution.py:1066
  144.9 0.7 copy-done.4
  145.6 31.4 %share.1 = (f32[50,768]{1,0:T(8,128)}, f32[1,1]{1,0:T(1,128)}) custom-call(f32[64,768]{1,0:T(8,128)} %copy-done.4, f32[50,768]{1,0:T(8,128)} %prompts.3), custom_call_target="tpu_custom_call" | custom-call | tf_op jit(solution)/shard_map/share/pallas_call | solution.py:1185
  177.1 0.0 copy-done.8
  177.1 0.0 copy-start.9
  177.1 1.2 copy.19
  178.3 0.0 copy-done.9
  178.3 0.7 copy.20
  (5 shorter events, 0.0 us)
Async XLA Ops:
  2.4 53.3 %copy-start.6 = (s32[7]{0:T(128)S(1)}, s32[7]{0:T(128)}, u32[]{:S(2)}) copy-start(s32[7]{0:T(128)} %groups.9) | copy-start | bytes 88
  62.1 1.2 copy-start
  63.3 0.7 copy-start.3
  119.8 10.3 %copy-start.5 = (f32[2,768]{1,0:T(2,128)S(1)}, f32[2,768]{1,0:T(2,128)}, u32[]{:S(2)}) copy-start(f32[2,768]{1,0:T(2,128)} %gains.5) | copy-start | bytes 18436
  119.8 10.3 %copy-start.7 = (s32[7]{0:T(128)S(1)}, s32[7]{0:T(128)}, u32[]{:S(2)}) copy-start(s32[7]{0:T(128)} %groups.9) | copy-start | bytes 88
  130.1 1.5 copy-start.1
  131.6 1.5 copy-start.2
  133.1 44.0 %copy-start.8 = (bf16[1152,768]{1,0:T(8,128)(2,1)S(1)}, bf16[1152,768]{1,0:T(8,128)(2,1)}, u32[]{:S(2)}) copy-start(bf16[1152,768]{1,0:T(8,128)(2,1)} %get-tuple-element.44) | copy-start | bytes 5308420
  144.9 0.7 copy-start.4
  177.1 1.2 copy-start.9
